TPU v7x, 32 devices: a whole 2x2x4 slice. The times are simulated.
32 devices in a mesh: scene: 4 (over y, core), seq: 8 (over z, x).
Axes of the slice: x: 2, y: 2, z: 4, core: 2. Of those that a mesh axis runs over, the one named last changes fastest.
Arguments:
- points: bfloat16 [32768, 256], P(('scene', 'seq')), may hold values from -100 to 100
- serial_rank: int32 [32768], P(('scene', 'seq')), may hold values from 0 to 8191, as said below
- mask_bits: int32 [12, 32768], P(None, ('scene', 'seq')), may hold values from 0 to 262143, as said below
- qkv_weight: bfloat16 [256, 768], replicated, may hold values from -2 to 2
- proj_weight: bfloat16 [256, 256], replicated, may hold values from -0.375 to 0.375
- up_weight: bfloat16 [256, 1024], replicated, may hold values from -0.375 to 0.375
- down_weight: bfloat16 [1024, 256], replicated, may hold values from -0.1875 to 0.1875
- queries: bfloat16 [200, 256], replicated, may hold values from -5 to 5
- dec_q_weight: bfloat16 [256, 256], replicated, may hold values from -3 to 3
- dec_kv_weight: bfloat16 [256, 512], replicated, may hold values from -2 to 2
- dec_out_weight: bfloat16 [256, 256], replicated, may hold values from -0.375 to 0.375
- mask_weight: bfloat16 [256, 256], replicated, may hold values from -0.375 to 0.375
Outputs:
- reserialized: bfloat16 [32768, 256], P(('scene', 'seq'))
- updated_queries: float32 [200, 256], replicated
- mask_logits: bfloat16 [200, 32768], P(None, ('scene', 'seq'))
Inputs may be any that keep to these rules, and one draw needn't show every extreme that they name: Within each scene group of 8192 points, serial_rank is a permutation of 0 to 8191. The points of one device have at most 256 ranks in any one range k * 1024 to (k + 1) * 1024 - 1, and in every draw that most is reached. `mask_bits`: word w holds the bits of queries 18 * w to 18 * w + 17 (the last word those that remain). In every block of 1024 points each query may attend to at least one point.
All inputs are finite; a program needn't handle non-finite values.
Results may differ from a plain program's by a relative error of at most 0.015.
Values may be sent and summed in bfloat16 or wider, within the bound.
A program may use at most 192 MiB of HBM per device.

v0:
```python
import math

import jax
import jax.numpy as jnp
from jax import lax
from jax.sharding import PartitionSpec as P

C = 256
HEADS = 16
HDIM = 16
PATCH = 1024
QUERIES = 200
DHEADS = 8
DHDIM = 32
WORDS = 12


def extended_2(cells, sides, width):
    for axis, dim in sides:
        count = lax.axis_size(axis)
        head = lax.slice_in_dim(cells, 0, width, axis=dim)
        tail = lax.slice_in_dim(cells, cells.shape[dim] - width, cells.shape[dim], axis=dim)
        cells = jnp.concatenate(
            [
                lax.ppermute(tail, axis, [(i, (i + 1) % count) for i in range(count)]),
                cells,
                lax.ppermute(head, axis, [((i + 1) % count, i) for i in range(count)]),
            ],
            axis=dim,
        )
    return cells


def merged_2(part, axis, combine):
    gathered = jax.tree.map(lambda a: lax.all_gather(a, axis), part)

    def take(source):
        return jax.tree.map(lambda a: lax.dynamic_index_in_dim(a, source, 0, False), gathered)

    return lax.fori_loop(
        1, lax.axis_size(axis), lambda source, state: combine(state, take(source)), take(0)
    )


def layer_norm(values):
    average = jnp.mean(values, axis=-1, keepdims=True)
    centered = values - average
    variance = jnp.mean(centered * centered, axis=-1, keepdims=True)
    return centered * lax.rsqrt(variance + 1e-05)


def head_group(triple):
    query_rows, key_rows, value_rows = triple
    scores = jnp.einsum(
        "qhd,khd->hqk", query_rows, key_rows, preferred_element_type=jnp.float32
    ) * (1.0 / math.sqrt(HDIM))
    weights = jax.nn.softmax(scores, axis=-1).astype(jnp.bfloat16)
    return jnp.einsum(
        "hqk,khd->qhd", weights, value_rows, preferred_element_type=jnp.float32
    ).astype(jnp.bfloat16)


def attend_half(pair):
    query_rows, joined = pair
    half_rows = query_rows.shape[0]
    groups = HEADS // 4
    query_groups = query_rows.reshape(half_rows, groups, 4, HDIM).transpose(1, 0, 2, 3)
    key_groups = joined[:, :C].reshape(PATCH, groups, 4, HDIM).transpose(1, 0, 2, 3)
    value_groups = joined[:, C:].reshape(PATCH, groups, 4, HDIM).transpose(1, 0, 2, 3)
    output = lax.map(head_group, (query_groups, key_groups, value_groups))
    return output.transpose(1, 0, 2, 3).reshape(half_rows, C)


def feed_forward(middle, up_weight, down_weight):
    normed_mid = layer_norm(middle.astype(jnp.float32)).astype(jnp.bfloat16)
    hidden_units = jax.nn.gelu(
        jnp.dot(normed_mid, up_weight, preferred_element_type=jnp.float32), approximate=True
    ).astype(jnp.bfloat16)
    return (
        middle.astype(jnp.float32)
        + jnp.dot(hidden_units, down_weight, preferred_element_type=jnp.float32)
    ).astype(jnp.bfloat16)


def reorder(point_rows, serial_rank):
    shard_rows = point_rows.shape[0]
    width = point_rows.shape[1]
    devices = lax.axis_size("seq")
    capacity = 2 * shard_rows // devices
    sorting = jnp.argsort(serial_rank)
    ranked = serial_rank[sorting]
    target = ranked // shard_rows
    matches = (target[:, None] == jnp.arange(devices, dtype=jnp.int32)[None, :]).astype(jnp.int32)
    counts = jnp.sum(matches, axis=0)
    starts = jnp.cumsum(counts) - counts
    within = jnp.arange(shard_rows, dtype=jnp.int32) - starts[target]
    outgoing = (
        jnp.zeros((devices, capacity, width), point_rows.dtype)
        .at[target, within]
        .set(point_rows[sorting])
    )
    slot_rank = (
        jnp.full((devices, capacity), shard_rows, jnp.int32)
        .at[target, within]
        .set(ranked % shard_rows)
    )
    arrived, arrived_slots = (
        lax.all_to_all(outgoing, "seq", split_axis=0, concat_axis=0, tiled=True),
        lax.all_to_all(slot_rank, "seq", split_axis=0, concat_axis=0, tiled=True),
    )
    placed = jnp.zeros((shard_rows, width), point_rows.dtype)
    return placed.at[arrived_slots.reshape(-1)].set(arrived.reshape(-1, width), mode="drop")


def unpack_bits(words):
    expanded = jnp.repeat(words, 18, axis=0)[:QUERIES]
    shifts = (jnp.arange(QUERIES, dtype=jnp.int32) % 18)[:, None]
    return jnp.right_shift(expanded, shifts) & 1 == 1


def combine(first, second):
    first_best, first_total, first_summed = first
    second_best, second_total, second_summed = second
    best = jnp.maximum(first_best, second_best)
    first_factor = jnp.exp(first_best - best)
    second_factor = jnp.exp(second_best - best)
    total = first_total * first_factor + second_total * second_factor
    summed = first_summed * first_factor[:, :, None] + second_summed * second_factor[:, :, None]
    return (best, total, summed)


def body(
    points,
    serial_rank,
    mask_bits,
    qkv_weight,
    proj_weight,
    up_weight,
    down_weight,
    queries,
    dec_q_weight,
    dec_kv_weight,
    dec_out_weight,
    mask_weight,
):
    shard_rows = points.shape[0]
    half_rows = PATCH // 2
    halves = shard_rows // half_rows
    normed = layer_norm(points.astype(jnp.float32)).astype(jnp.bfloat16)
    projected = jnp.dot(normed, qkv_weight, preferred_element_type=jnp.float32).astype(jnp.bfloat16)
    query_rows = projected[:, :C].reshape(halves, half_rows, C)
    key_value = projected[:, C:]
    extended = extended_2(key_value, (("seq", 0),), half_rows)
    own_half = key_value.reshape(halves, half_rows, 2 * C)
    prev_half = extended[:shard_rows].reshape(halves, half_rows, 2 * C)
    next_half = extended[2 * half_rows :].reshape(halves, half_rows, 2 * C)
    first_half = lax.axis_index("seq") * halves
    odd_half = (first_half + jnp.arange(halves, dtype=jnp.int32)) % 2 == 1
    partner = jnp.where(odd_half[:, None, None], next_half, prev_half)
    joined = jnp.concatenate([own_half, partner], axis=1)
    attended = lax.map(attend_half, (query_rows, joined)).reshape(shard_rows, C)
    middle = (
        points.astype(jnp.float32)
        + jnp.dot(attended, proj_weight, preferred_element_type=jnp.float32)
    ).astype(jnp.bfloat16)
    block_out = feed_forward(middle, up_weight, down_weight)
    reserialized = reorder(block_out, serial_rank)
    point_norm = layer_norm(block_out.astype(jnp.float32)).astype(jnp.bfloat16)
    dec_rows = jnp.dot(point_norm, dec_kv_weight, preferred_element_type=jnp.float32).astype(
        jnp.bfloat16
    )
    query_heads = jnp.dot(queries, dec_q_weight, preferred_element_type=jnp.float32).astype(
        jnp.bfloat16
    )
    query_heads = query_heads.reshape(QUERIES, DHEADS, DHDIM)
    width = min(512, shard_rows)
    block_count = shard_rows // width
    row_blocks = dec_rows.reshape(block_count, width, 2 * C)
    word_blocks = mask_bits.reshape(WORDS, block_count, width).transpose(1, 0, 2)
    scale = 1.0 / math.sqrt(DHDIM)

    def accumulate(carry, pieces):
        best, total, summed = carry
        rows_block, words_block = pieces
        key_rows = rows_block[:, :C].reshape(width, DHEADS, DHDIM)
        value_rows = rows_block[:, C:].reshape(width, DHEADS, DHDIM).astype(jnp.float32)
        allowed = unpack_bits(words_block)[None, :, :]
        scores = (
            jnp.einsum("qhd,khd->hqk", query_heads, key_rows, preferred_element_type=jnp.float32)
            * scale
        )
        scores = jnp.where(allowed, scores, jnp.float32(-1e30))
        new_best = jnp.maximum(best, jnp.max(scores, axis=-1))
        weights = jnp.where(allowed, jnp.exp(scores - new_best[:, :, None]), jnp.float32(0.0))
        factor = jnp.exp(best - new_best)
        total = total * factor + jnp.sum(weights, axis=-1)
        summed = summed * factor[:, :, None] + jnp.einsum(
            "hqk,khd->hqd", weights, value_rows, precision=lax.Precision.HIGHEST
        )
        return ((new_best, total, summed), None)

    start = (
        jnp.full((DHEADS, QUERIES), -1e30, jnp.float32),
        jnp.zeros((DHEADS, QUERIES), jnp.float32),
        jnp.zeros((DHEADS, QUERIES, DHDIM), jnp.float32),
    )
    partial_sums, unused = lax.scan(accumulate, start, (row_blocks, word_blocks))
    group_sums = merged_2(partial_sums, "seq", combine)
    merged = merged_2(group_sums, "scene", combine)
    best, total, summed = merged
    cross = (summed / total[:, :, None]).transpose(1, 0, 2).reshape(QUERIES, C).astype(jnp.bfloat16)
    updated = layer_norm(
        queries.astype(jnp.float32)
        + jnp.dot(cross, dec_out_weight, preferred_element_type=jnp.float32)
    )
    embed = jnp.dot(
        updated.astype(jnp.bfloat16), mask_weight, preferred_element_type=jnp.float32
    ).astype(jnp.bfloat16)
    logits = lax.dot_general(
        embed, point_norm, (((1,), (1,)), ((), ())), preferred_element_type=jnp.float32
    )
    logits = (logits * (1.0 / math.sqrt(C))).astype(jnp.bfloat16)
    return (reserialized, updated, logits)


def solution(mesh):
    in_specs = (
        P(("scene", "seq"), None),
        P(("scene", "seq")),
        P(None, ("scene", "seq")),
        P(),
        P(),
        P(),
        P(),
        P(),
        P(),
        P(),
        P(),
        P(),
    )
    out_specs = (P(("scene", "seq"), None), P(), P(None, ("scene", "seq")))
    return jax.shard_map(body, mesh=mesh, in_specs=in_specs, out_specs=out_specs, check_vma=False)
```

profile of v0, /device:TPU:1, one launch (start us, length us, event | category | flops | bytes accessed | tf_op | source)
XLA Modules:
  0.0 324.4 jit_solution(14926656123037931306)
XLA Ops:
  7.2 1.3 copy.54
  8.8 1.6 convolution_convert_fusion
  10.6 5.1 %collective-permute-start = (bf16[512,512]{1,0:T(8,128)(2,1)S(1)}, bf16[512,512]{1,0:T(8,128)(2,1)S(1)}, u32[]{:S(2)}, u32[]{:S(2)}) collective-permute-start(bf16[512,512]{1,0:T(8,128)(2,1)S(1)} %get-tuple-element.699), channel_id=1, source_target_pairs={{1,0},{2,1},{3,2},{4,3},{5,4},{6,5},{7,6},{0,7},{9,8},{10,9},{11,1... | collective-permute-start | bytes 1572872 | tf_op jit(solution)/shard_map/ppermute | solution.py:27
  16.6 1.3 copy.57
  19.6 4.4 %sort.17 = (s32[1024]{0:T(1024)}, s32[1024]{0:T(1024)S(1)}) sort(s32[1024]{0:T(1024)S(1)} %copy-done.1, s32[1024]{0:T(1024)S(1)} %iota.25), dimensions={0}, to_apply=%region_0.0 | sort | flops 10240 | bytes 16384 | tf_op jit(solution)/shard_map/jit(argsort)/sort | solution.py:90
  24.0 4.5 %gather_fusion = s32[1024]{0:T(1024)S(1)} fusion(s32[1024]{0:T(1024)S(1)} %copy-done.1, s32[1024]{0:T(1024)S(1)} %fusion.132), kind=kCustom, calls=%fused_computation | custom fusion | bytes 12288 | tf_op jit(solution)/shard_map/gather | solution.py:91
  30.1 5.4 %collective-permute-done = bf16[512,512]{1,0:T(8,128)(2,1)S(1)} collective-permute-done((bf16[512,512]{1,0:T(8,128)(2,1)S(1)}, bf16[512,512]{1,0:T(8,128)(2,1)S(1)}, u32[]{:S(2)}, u32[]{:S(2)}) %collective-permute-start) | collective-permute-done | bytes 524320 | tf_op jit(solution)/shard_map/ppermute | solution.py:27
  36.5 2.1 pad_maximum_fusion.1
  39.1 1.5 copy.56
  40.8 1.0 copy-done.7
  42.2 70.8 %while.76 = (s32[]{:T(128)}, bf16[2,512,256]{2,1,0:T(8,128)(2,1)}, bf16[2,512,256]{2,1,0:T(8,128)(2,1)}, bf16[2,1024,512]{1,2,0:T(8,128)(2,1)S(1)}, s32[]{:T(128)}, /*index=5*/s32[]{:T(128)}, s32[]{:T(128)}) while((s32[]{:T(128)}, bf16[2,512,256]{2,1,0:T(8,128)(2,1)}, bf16[2,512,256]{2,1,0:T(8,128)(2,1)}, ...), condition=%wide.region_11.12_spmd, body=%wide.region_6.11_spmd.sunk | while | flops 216043520 | bytes 8998638 | solution.py:161
  42.3 1.0 fusion.197
  44.2 31.6 %while.80 = (s32[]{:T(128)}, bf16[4,512,4,16]{1,3,2,0:T(8,128)(2,1)}, bf16[4,1024,4,16]{1,3,2,0:T(8,128)(2,1)}, bf16[4,512,4,16]{1,3,2,0:T(8,128)(2,1)}, bf16[4,1024,4,16]{1,3,2,0:T(8,128)(2,1)}, /*index=5*/s32[]{:T(128)}) while((s32[]{:T(128)}, bf16[4,512,4,16]{1,3,2,0:T(8,128)(2,1)}, bf16[4,1024,4,16]{1,3,2,0:T(8,128)(2,1)}, ...), condition=%wide.region_10.10_spmd, body=%wide.region_7.9_spmd.sunk | while | flops 216043520 | bytes 609349 | solution.py:70
  44.2 3.4 %fusion.217 = f32[4,512]{1,0:T(4,128)S(1)} fusion(bf16[4,1024,4,16]{1,3,2,0:T(8,128)(2,1)} %get-tuple-element.964, s32[]{:T(128)} %get-tuple-element.954, bf16[4,512,4,16]{1,3,2,0:T(8,128)(2,1)} %get-tuple-element.963), kind=kOutput, calls=%fused_computation.188.clone.1 | convolution fusion | flops 73401344 | bytes 205824 | tf_op jit(solution)/shard_map/while/body/eval_jaxpr/while/body/eval_jaxpr/sub | solution.py:57
  47.6 4.5 %fusion.218 = bf16[4,512,4,16]{1,3,2,0:T(8,128)(2,1)} fusion(bf16[4,512,4,16]{1,3,2,0:T(8,128)(2,1)} %get-tuple-element.955, s32[]{:T(128)} %get-tuple-element.954, f32[4,512]{1,0:T(4,128)S(1)} %fusion.217, bf16[4,1024,4,16]{1,3,2,0:T(8,128)(2,1)} %get-tuple-element.962, bf16[4,1024,4,16]{1,3,2,0:T(8,128)(2,1)} %get-tuple-element.964, ...), kind=kOutput, calls=%fused_computation.14.clone.1 | convolution fusion | flops 142642176 | bytes 403456 | tf_op jit(solution)/shard_map/while/body/eval_jaxpr/while/body/eval_jaxpr/hqk,khd->qhd/dot_general | solution.py:58
  52.1 3.4 %fusion.217 = f32[4,512]{1,0:T(4,128)S(1)} fusion(bf16[4,1024,4,16]{1,3,2,0:T(8,128)(2,1)} %get-tuple-element.964, s32[]{:T(128)} %get-tuple-element.954, bf16[4,512,4,16]{1,3,2,0:T(8,128)(2,1)} %get-tuple-element.963), kind=kOutput, calls=%fused_computation.188.clone.1 | convolution fusion | flops 73401344 | bytes 205824 | tf_op jit(solution)/shard_map/while/body/eval_jaxpr/while/body/eval_jaxpr/sub | solution.py:57
  55.5 4.5 %fusion.218 = bf16[4,512,4,16]{1,3,2,0:T(8,128)(2,1)} fusion(bf16[4,512,4,16]{1,3,2,0:T(8,128)(2,1)} %get-tuple-element.955, s32[]{:T(128)} %get-tuple-element.954, f32[4,512]{1,0:T(4,128)S(1)} %fusion.217, bf16[4,1024,4,16]{1,3,2,0:T(8,128)(2,1)} %get-tuple-element.962, bf16[4,1024,4,16]{1,3,2,0:T(8,128)(2,1)} %get-tuple-element.964, ...), kind=kOutput, calls=%fused_computation.14.clone.1 | convolution fusion | flops 142642176 | bytes 403456 | tf_op jit(solution)/shard_map/while/body/eval_jaxpr/while/body/eval_jaxpr/hqk,khd->qhd/dot_general | solution.py:58
  60.0 3.4 %fusion.217 = f32[4,512]{1,0:T(4,128)S(1)} fusion(bf16[4,1024,4,16]{1,3,2,0:T(8,128)(2,1)} %get-tuple-element.964, s32[]{:T(128)} %get-tuple-element.954, bf16[4,512,4,16]{1,3,2,0:T(8,128)(2,1)} %get-tuple-element.963), kind=kOutput, calls=%fused_computation.188.clone.1 | convolution fusion | flops 73401344 | bytes 205824 | tf_op jit(solution)/shard_map/while/body/eval_jaxpr/while/body/eval_jaxpr/sub | solution.py:57
  63.4 4.5 %fusion.218 = bf16[4,512,4,16]{1,3,2,0:T(8,128)(2,1)} fusion(bf16[4,512,4,16]{1,3,2,0:T(8,128)(2,1)} %get-tuple-element.955, s32[]{:T(128)} %get-tuple-element.954, f32[4,512]{1,0:T(4,128)S(1)} %fusion.217, bf16[4,1024,4,16]{1,3,2,0:T(8,128)(2,1)} %get-tuple-element.962, bf16[4,1024,4,16]{1,3,2,0:T(8,128)(2,1)} %get-tuple-element.964, ...), kind=kOutput, calls=%fused_computation.14.clone.1 | convolution fusion | flops 142642176 | bytes 403456 | tf_op jit(solution)/shard_map/while/body/eval_jaxpr/while/body/eval_jaxpr/hqk,khd->qhd/dot_general | solution.py:58
  67.9 3.4 %fusion.217 = f32[4,512]{1,0:T(4,128)S(1)} fusion(bf16[4,1024,4,16]{1,3,2,0:T(8,128)(2,1)} %get-tuple-element.964, s32[]{:T(128)} %get-tuple-element.954, bf16[4,512,4,16]{1,3,2,0:T(8,128)(2,1)} %get-tuple-element.963), kind=kOutput, calls=%fused_computation.188.clone.1 | convolution fusion | flops 73401344 | bytes 205824 | tf_op jit(solution)/shard_map/while/body/eval_jaxpr/while/body/eval_jaxpr/sub | solution.py:57
  71.3 4.5 %fusion.218 = bf16[4,512,4,16]{1,3,2,0:T(8,128)(2,1)} fusion(bf16[4,512,4,16]{1,3,2,0:T(8,128)(2,1)} %get-tuple-element.955, s32[]{:T(128)} %get-tuple-element.954, f32[4,512]{1,0:T(4,128)S(1)} %fusion.217, bf16[4,1024,4,16]{1,3,2,0:T(8,128)(2,1)} %get-tuple-element.962, bf16[4,1024,4,16]{1,3,2,0:T(8,128)(2,1)} %get-tuple-element.964, ...), kind=kOutput, calls=%fused_computation.14.clone.1 | convolution fusion | flops 142642176 | bytes 403456 | tf_op jit(solution)/shard_map/while/body/eval_jaxpr/while/body/eval_jaxpr/hqk,khd->qhd/dot_general | solution.py:58
  75.8 1.1 copy.86
  77.7 1.0 fusion.197
  79.6 31.6 %while.80 = (s32[]{:T(128)}, bf16[4,512,4,16]{1,3,2,0:T(8,128)(2,1)}, bf16[4,1024,4,16]{1,3,2,0:T(8,128)(2,1)}, bf16[4,512,4,16]{1,3,2,0:T(8,128)(2,1)}, bf16[4,1024,4,16]{1,3,2,0:T(8,128)(2,1)}, /*index=5*/s32[]{:T(128)}) while((s32[]{:T(128)}, bf16[4,512,4,16]{1,3,2,0:T(8,128)(2,1)}, bf16[4,1024,4,16]{1,3,2,0:T(8,128)(2,1)}, ...), condition=%wide.region_10.10_spmd, body=%wide.region_7.9_spmd.sunk | while | flops 216043520 | bytes 609349 | solution.py:70
  79.6 3.4 %fusion.217 = f32[4,512]{1,0:T(4,128)S(1)} fusion(bf16[4,1024,4,16]{1,3,2,0:T(8,128)(2,1)} %get-tuple-element.964, s32[]{:T(128)} %get-tuple-element.954, bf16[4,512,4,16]{1,3,2,0:T(8,128)(2,1)} %get-tuple-element.963), kind=kOutput, calls=%fused_computation.188.clone.1 | convolution fusion | flops 73401344 | bytes 205824 | tf_op jit(solution)/shard_map/while/body/eval_jaxpr/while/body/eval_jaxpr/sub | solution.py:57
  83.0 4.5 %fusion.218 = bf16[4,512,4,16]{1,3,2,0:T(8,128)(2,1)} fusion(bf16[4,512,4,16]{1,3,2,0:T(8,128)(2,1)} %get-tuple-element.955, s32[]{:T(128)} %get-tuple-element.954, f32[4,512]{1,0:T(4,128)S(1)} %fusion.217, bf16[4,1024,4,16]{1,3,2,0:T(8,128)(2,1)} %get-tuple-element.962, bf16[4,1024,4,16]{1,3,2,0:T(8,128)(2,1)} %get-tuple-element.964, ...), kind=kOutput, calls=%fused_computation.14.clone.1 | convolution fusion | flops 142642176 | bytes 403456 | tf_op jit(solution)/shard_map/while/body/eval_jaxpr/while/body/eval_jaxpr/hqk,khd->qhd/dot_general | solution.py:58
  87.5 3.4 %fusion.217 = f32[4,512]{1,0:T(4,128)S(1)} fusion(bf16[4,1024,4,16]{1,3,2,0:T(8,128)(2,1)} %get-tuple-element.964, s32[]{:T(128)} %get-tuple-element.954, bf16[4,512,4,16]{1,3,2,0:T(8,128)(2,1)} %get-tuple-element.963), kind=kOutput, calls=%fused_computation.188.clone.1 | convolution fusion | flops 73401344 | bytes 205824 | tf_op jit(solution)/shard_map/while/body/eval_jaxpr/while/body/eval_jaxpr/sub | solution.py:57
  90.9 4.5 %fusion.218 = bf16[4,512,4,16]{1,3,2,0:T(8,128)(2,1)} fusion(bf16[4,512,4,16]{1,3,2,0:T(8,128)(2,1)} %get-tuple-element.955, s32[]{:T(128)} %get-tuple-element.954, f32[4,512]{1,0:T(4,128)S(1)} %fusion.217, bf16[4,1024,4,16]{1,3,2,0:T(8,128)(2,1)} %get-tuple-element.962, bf16[4,1024,4,16]{1,3,2,0:T(8,128)(2,1)} %get-tuple-element.964, ...), kind=kOutput, calls=%fused_computation.14.clone.1 | convolution fusion | flops 142642176 | bytes 403456 | tf_op jit(solution)/shard_map/while/body/eval_jaxpr/while/body/eval_jaxpr/hqk,khd->qhd/dot_general | solution.py:58
  95.4 3.4 %fusion.217 = f32[4,512]{1,0:T(4,128)S(1)} fusion(bf16[4,1024,4,16]{1,3,2,0:T(8,128)(2,1)} %get-tuple-element.964, s32[]{:T(128)} %get-tuple-element.954, bf16[4,512,4,16]{1,3,2,0:T(8,128)(2,1)} %get-tuple-element.963), kind=kOutput, calls=%fused_computation.188.clone.1 | convolution fusion | flops 73401344 | bytes 205824 | tf_op jit(solution)/shard_map/while/body/eval_jaxpr/while/body/eval_jaxpr/sub | solution.py:57
  98.8 4.5 %fusion.218 = bf16[4,512,4,16]{1,3,2,0:T(8,128)(2,1)} fusion(bf16[4,512,4,16]{1,3,2,0:T(8,128)(2,1)} %get-tuple-element.955, s32[]{:T(128)} %get-tuple-element.954, f32[4,512]{1,0:T(4,128)S(1)} %fusion.217, bf16[4,1024,4,16]{1,3,2,0:T(8,128)(2,1)} %get-tuple-element.962, bf16[4,1024,4,16]{1,3,2,0:T(8,128)(2,1)} %get-tuple-element.964, ...), kind=kOutput, calls=%fused_computation.14.clone.1 | convolution fusion | flops 142642176 | bytes 403456 | tf_op jit(solution)/shard_map/while/body/eval_jaxpr/while/body/eval_jaxpr/hqk,khd->qhd/dot_general | solution.py:58
  103.3 3.4 %fusion.217 = f32[4,512]{1,0:T(4,128)S(1)} fusion(bf16[4,1024,4,16]{1,3,2,0:T(8,128)(2,1)} %get-tuple-element.964, s32[]{:T(128)} %get-tuple-element.954, bf16[4,512,4,16]{1,3,2,0:T(8,128)(2,1)} %get-tuple-element.963), kind=kOutput, calls=%fused_computation.188.clone.1 | convolution fusion | flops 73401344 | bytes 205824 | tf_op jit(solution)/shard_map/while/body/eval_jaxpr/while/body/eval_jaxpr/sub | solution.py:57
  106.7 4.5 %fusion.218 = bf16[4,512,4,16]{1,3,2,0:T(8,128)(2,1)} fusion(bf16[4,512,4,16]{1,3,2,0:T(8,128)(2,1)} %get-tuple-element.955, s32[]{:T(128)} %get-tuple-element.954, f32[4,512]{1,0:T(4,128)S(1)} %fusion.217, bf16[4,1024,4,16]{1,3,2,0:T(8,128)(2,1)} %get-tuple-element.962, bf16[4,1024,4,16]{1,3,2,0:T(8,128)(2,1)} %get-tuple-element.964, ...), kind=kOutput, calls=%fused_computation.14.clone.1 | convolution fusion | flops 142642176 | bytes 403456 | tf_op jit(solution)/shard_map/while/body/eval_jaxpr/while/body/eval_jaxpr/hqk,khd->qhd/dot_general | solution.py:58
  111.2 1.1 copy.86
  113.0 1.4 convert_reduce_fusion
  114.6 3.1 convert_reduce_fusion.2
  118.5 19.2 %while.79 = (s32[]{:T(128)}, f32[8,200]{1,0:T(8,128)S(1)}, f32[8,200]{1,0:T(8,128)S(1)}, f32[8,200,32]{1,2,0:T(8,128)}, s32[2,12,512]{2,0,1:T(2,128)S(1)}, /*ind...) while((s32[]{:T(128)}, f32[8,200]{1,0:T(8,128)S(1)}, ...), condition=%wide.region_21.22_spmd.clone, body=%wide.region_18.21_spmd.clone.sunk | while | flops 377302016 | bytes 31131396 | solution.py:207
  119.4 2.4 fusion.207
  121.8 3.1 fusion.208
  124.9 2.6 fusion.210
  128.9 2.4 fusion.207
  131.3 3.1 fusion.208
  134.4 2.6 fusion.210
  137.8 4.4 %compare_select_fusion.3 = (s32[1024,1]{0,1:T(1,128)S(1)}, s32[1024,1]{0,1:T(1,128)S(1)}) fusion(s32[]{:T(128)} %bitcast.24, s32[]{:T(128)} %bitcast.25, s32[]{:T(128)} %bitcast.26, s32[]{:T(128)} %bitcast.27, s32[]{:T(128)} %bitcast.28, s32[]{:T(128)} %bitcast.30, s32[]{:T(128)} %bitcast.29, s32[1024,1]{0,1:T(1,128)S(1)} %bitcast.233), kind=kLoop, calls=%fused_computation.143 | loop fusion | flops 30720 | bytes 12316 | tf_op jit(solution)/shard_map/gather | solution.py:96
  143.0 5.0 %scatter_custom_fusion.1 = s32[2048]{0:T(1024)} fusion(s32[1024]{0:T(1024)S(1)} %broadcast_select_fusion.2, s32[1024]{0:T(1024)} %get-tuple-element.702, s32[]{:T(128)} %constant.261.clone.1), kind=kCustom, calls=%fused_computation.163 | custom fusion | bytes 8704
  148.1 4.6 %all-to-all-start = ((s32[8,1,256]{2,1,0:T(1,128)}), s32[8,1,256]{2,1,0:T(1,128)S(1)}, u32[]{:S(2)}, u32[]{:S(2)}) async-start(s32[8,1,256]{2,1,0:T(1,128)} %bitcast.33), calls=%async_computation | async-start | bytes 16384 | tf_op jit(solution)/shard_map/all_to_all | solution.py:109
  152.9 9.4 %scatter_custom_fusion.2 = bf16[2048,256]{1,0:T(8,128)(2,1)} fusion(s32[1024]{0:T(1024)S(1)} %broadcast_select_fusion.2, bf16[1024,256]{1,0:T(8,128)(2,1)S(1)} %copy.60, s32[1024]{0:T(1024)} %copy-done.21, bf16[]{:T(256)} %constant.260.clone.1), kind=kCustom, calls=%fused_computation.124 | custom fusion | bytes 1049088
  162.4 5.4 %all-to-all-start.1 = ((bf16[8,256,256]{2,1,0:T(8,128)(2,1)}), bf16[8,256,256]{2,1,0:T(8,128)(2,1)S(1)}, u32[]{:S(2)}, u32[]{:S(2)}) async-start(bf16[8,256,256]{2,1,0:T(8,128)(2,1)} %bitcast.41), calls=%async_computation.1 | async-start | bytes 2097152 | tf_op jit(solution)/shard_map/all_to_all | solution.py:108
  167.8 55.7 %all-gather = f32[64,200]{1,0:T(8,128)S(1)} all-gather(f32[8,200]{1,0:T(8,128)S(1)} %get-tuple-element.502), channel_id=2, replica_groups=mesh['scene'=4,'seq'=8] {'seq'}, dimensions={0}, use_global_device_ids=true | all-gather | bytes 57600 | tf_op jit(solution)/shard_map/all_gather | solution.py:35
  223.5 24.4 %all-gather.1 = f32[64,200]{1,0:T(8,128)S(1)} all-gather(f32[8,200]{1,0:T(8,128)S(1)} %get-tuple-element.503), channel_id=3, replica_groups=mesh['scene'=4,'seq'=8] {'seq'}, dimensions={0}, use_global_device_ids=true | all-gather | bytes 57600 | tf_op jit(solution)/shard_map/all_gather | solution.py:35
  248.0 10.2 %scatter_custom_fusion = bf16[1024,256]{1,0:T(8,128)(2,1)} fusion(s32[2048]{0:T(1024)S(1)} %bitcast.237, bf16[2048,256]{1,0:T(8,128)(2,1)S(1)} %bitcast.226, bf16[]{:T(256)} %constant.260.clone.1), kind=kCustom, calls=%fused_computation.132 | custom fusion | bytes 524290 | tf_op jit(solution)/shard_map/scatter | solution.py:112
  259.4 14.2 %while.77 = (s32[]{:T(128)}, f32[8,200]{1,0:T(8,128)S(1)}, f32[8,200]{1,0:T(8,128)S(1)}, f32[8,200,32]{2,1,0:T(8,128)S(1)}, f32[8,8,200]{2,1,0:T(8,128)S(1)}, /*...) while((s32[]{:T(128)}, f32[8,200]{1,0:T(8,128)S(1)}, ...), condition=%wide.region_23.24_spmd, body=%wide.region_22.23_spmd.sunk | while | flops 163205 | bytes 1497751 | solution.py:40
  259.5 1.0 constant_dynamic-slice_fusion.11
  261.5 1.0 constant_dynamic-slice_fusion.11
  263.6 1.0 constant_dynamic-slice_fusion.11
  265.6 1.0 constant_dynamic-slice_fusion.11
  267.6 1.0 constant_dynamic-slice_fusion.11
  269.7 1.0 constant_dynamic-slice_fusion.11
  271.7 1.0 constant_dynamic-slice_fusion.11
  274.0 21.9 %all-gather.5 = f32[32,200,32]{1,2,0:T(8,128)S(1)} all-gather(f32[8,200,32]{1,2,0:T(8,128)S(1)} %copy.66), channel_id=7, replica_groups=mesh['scene'=4,'seq'=8] {'scene'}, dimensions={0}, use_global_device_ids=true | all-gather | bytes 1024000 | tf_op jit(solution)/shard_map/all_gather | solution.py:35
  296.2 5.2 %all-gather.3 = f32[32,200]{1,0:T(8,128)S(1)} all-gather(f32[8,200]{1,0:T(8,128)S(1)} %get-tuple-element.505), channel_id=5, replica_groups=mesh['scene'=4,'seq'=8] {'scene'}, dimensions={0}, use_global_device_ids=true | all-gather | bytes 32000 | tf_op jit(solution)/shard_map/all_gather | solution.py:35
  301.4 5.6 %all-gather.4 = f32[32,200]{1,0:T(8,128)} all-gather(f32[8,200]{1,0:T(8,128)S(1)} %get-tuple-element.506), channel_id=6, replica_groups=mesh['scene'=4,'seq'=8] {'scene'}, dimensions={0}, use_global_device_ids=true | all-gather | bytes 32000 | tf_op jit(solution)/shard_map/all_gather | solution.py:35
  307.7 5.3 %while.78 = (s32[]{:T(128)}, f32[8,200]{1,0:T(8,128)S(1)}, f32[8,200]{1,0:T(8,128)S(1)}, f32[8,200,32]{2,1,0:T(8,128)S(1)}, f32[4,8,200]{2,1,0:T(8,128)S(1)}, /*...) while((s32[]{:T(128)}, f32[8,200]{1,0:T(8,128)S(1)}, ...), condition=%wide.region_25.26_spmd, body=%wide.region_24.25_spmd.sunk | while | flops 163205 | bytes 1497751 | solution.py:40
  313.5 1.3 fusion.160
  315.2 2.4 fusion.100
  (186 shorter events, 30.1 us)
Async XLA Ops:
  7.2 107.4 %copy-start = (bf16[1024,256]{1,0:T(8,128)(2,1)S(1)}, bf16[1024,256]{1,0:T(8,128)(2,1)}, u32[]{:S(2)}) copy-start(bf16[1024,256]{1,0:T(8,128)(2,1)} %param.28) | copy-start | bytes 1572868
  7.2 251.0 %all-gather.8.cloned.1.call-start = ((), (), s32[]{:S(2)}) async-start(), calls=%async_computation.2 | async-start | bytes 2359296 | tf_op jit(solution)/shard_map/all_gather | solution.py:35
  8.5 1.9 copy-start.3
  10.5 7.5 %copy-start.11 = (bf16[200,256]{1,0:T(8,128)(2,1)S(1)}, bf16[200,256]{1,0:T(8,128)(2,1)}, u32[]{:S(2)}) copy-start(bf16[200,256]{1,0:T(8,128)(2,1)} %param.29) | copy-start | bytes 307204
  10.5 7.5 %copy-start.16 = (bf16[256,256]{1,0:T(8,128)(2,1)S(1)}, bf16[256,256]{1,0:T(8,128)(2,1)}, u32[]{:S(2)}) copy-start(bf16[256,256]{1,0:T(8,128)(2,1)} %param.30) | copy-start | bytes 393220
  10.6 8.4 %copy-start.18 = (s32[12,1024]{1,0:T(8,128)S(1)}, s32[12,1024]{1,0:T(8,128)}, u32[]{:S(2)}) copy-start(s32[12,1024]{1,0:T(8,128)} %param.24) | copy-start | bytes 147460
  10.6 9.0 %copy-start.1 = (s32[1024]{0:T(1024)S(1)}, s32[1024]{0:T(1024)}, u32[]{:S(2)}) copy-start(s32[1024]{0:T(1024)} %param.23) | copy-start | bytes 12292
  10.6 24.9 %collective-permute-start = (bf16[512,512]{1,0:T(8,128)(2,1)S(1)}, bf16[512,512]{1,0:T(8,128)(2,1)S(1)}, u32[]{:S(2)}, u32[]{:S(2)}) collective-permute-start(bf16[512,512]{1,0:T(8,128)(2,1)S(1)} %get-tuple-element.699), channel_id=1, source_target_pairs={{1,0},{2,1},{3,2},{4,3},{5,4},{6,5},{7,6},{0,7},{9,8},{10,9},{11,1... | collective-permute-start | bytes 1572872 | tf_op jit(solution)/shard_map/ppermute | solution.py:27
  15.7 20.7 %collective-permute-start.1 = (bf16[512,512]{1,0:T(8,128)(2,1)S(1)}, bf16[512,512]{1,0:T(8,128)(2,1)}, u32[]{:S(2)}, u32[]{:S(2)}) collective-permute-start(bf16[512,512]{1,0:T(8,128)(2,1)S(1)} %get-tuple-element.698), channel_id=1, source_target_pairs={{0,1},{1,2},{2,3},{3,4},{4,5},{5,6},{6,7},{7,0},{8,9},{9,10},{10,1... | collective-permute-start | bytes 1572872 | tf_op jit(solution)/shard_map/ppermute | solution.py:25
  24.0 14.6 %copy-start.21 = (s32[1024]{0:T(1024)}, s32[1024]{0:T(1024)S(1)}, u32[]{:S(2)}) copy-start(s32[1024]{0:T(1024)S(1)} %fusion.132) | copy-start | bytes 12292
  28.5 12.1 %copy-start.19 = (s32[1024]{0:T(1024)}, s32[1024]{0:T(1024)S(1)}, u32[]{:S(2)}) copy-start(s32[1024]{0:T(1024)S(1)} %gather_fusion) | copy-start | bytes 12292
  40.7 1.2 copy-start.7
  42.1 70.8 %copy-start.4 = (bf16[1024,256]{0,1:T(8,128)(2,1)S(1)}, bf16[1024,256]{0,1:T(8,128)(2,1)}, u32[]{:S(2)}) copy-start(bf16[1024,256]{0,1:T(8,128)(2,1)} %copy-done.3) | copy-start | bytes 1572868
  42.2 70.8 %copy-start.17 = (bf16[256,256]{1,0:T(8,128)(2,1)S(1)}, bf16[256,256]{1,0:T(8,128)(2,1)}, u32[]{:S(2)}) copy-start(bf16[256,256]{1,0:T(8,128)(2,1)} %param.26) | copy-start | bytes 393220
  42.2 1.2 copy-start.5
  77.6 1.1 copy-start.5
  114.6 3.3 %copy-start.24 = (bf16[256,512]{1,0:T(8,128)(2,1)S(1)}, bf16[256,512]{1,0:T(8,128)(2,1)}, u32[]{:S(2)}) copy-start(bf16[256,512]{1,0:T(8,128)(2,1)} %param.31) | copy-start | bytes 786436
  114.6 3.8 %copy-start.6 = (bf16[200,256]{0,1:T(8,128)(2,1)S(1)}, bf16[200,256]{0,1:T(8,128)(2,1)}, u32[]{:S(2)}) copy-start(bf16[200,256]{0,1:T(8,128)(2,1)} %copy.61) | copy-start | bytes 307204
  114.6 3.8 %copy-start.9 = (f32[8,200]{1,0:T(8,128)S(1)}, f32[8,200]{1,0:T(8,128)}, u32[]{:S(2)}) copy-start(f32[8,200]{1,0:T(8,128)} %custom-call) | copy-start | bytes 19204
  114.6 3.8 %copy-start.10 = (s32[12,2,512]{2,1,0:T(2,128)S(1)}, s32[12,2,512]{2,1,0:T(2,128)}, u32[]{:S(2)}) copy-start(s32[12,2,512]{2,1,0:T(2,128)} %reshape.297) | copy-start | bytes 147460
  114.6 3.8 %copy-start.12 = (f32[8,200]{1,0:T(8,128)S(1)}, f32[8,200]{1,0:T(8,128)}, u32[]{:S(2)}) copy-start(f32[8,200]{1,0:T(8,128)} %custom-call.1) | copy-start | bytes 19204
  117.7 35.0 %copy-start.8 = (bf16[1024,256]{0,1:T(8,128)(2,1)}, bf16[1024,256]{0,1:T(8,128)(2,1)S(1)}, u32[]{:S(2)}) copy-start(bf16[1024,256]{0,1:T(8,128)(2,1)S(1)} %get-tuple-element.715) | copy-start | bytes 1572868
  118.5 19.3 %copy-start.20 = (s32[1024]{0:T(1024)S(1)}, s32[1024]{0:T(1024)}, u32[]{:S(2)}) copy-start(s32[1024]{0:T(1024)} %copy-done.19) | copy-start | bytes 12292
  118.5 24.4 %copy-start.23 = (s32[2]{0:T(128)S(1)}, s32[2]{0:T(128)}, u32[]{:S(2)}) copy-start(s32[2]{0:T(128)} %constant.280) | copy-start | bytes 28
  118.5 24.5 %copy-start.22 = (s32[2]{0:T(128)S(1)}, s32[2]{0:T(128)}, u32[]{:S(2)}) copy-start(s32[2]{0:T(128)} %constant.283) | copy-start | bytes 28
  119.3 5.6 %copy-start.13 = (f32[8,200,32]{1,2,0:T(8,128)S(1)}, f32[8,200,32]{1,2,0:T(8,128)}, u32[]{:S(2)}) copy-start(f32[8,200,32]{1,2,0:T(8,128)} %get-tuple-element.999) | copy-start | bytes 614404 | tf_op jit(solution)/shard_map/while
  121.8 3.1 copy-start.2
  127.5 0.7 copy-start.14
  128.9 5.6 %copy-start.13 = (f32[8,200,32]{1,2,0:T(8,128)S(1)}, f32[8,200,32]{1,2,0:T(8,128)}, u32[]{:S(2)}) copy-start(f32[8,200,32]{1,2,0:T(8,128)} %get-tuple-element.999) | copy-start | bytes 614404 | tf_op jit(solution)/shard_map/while
  131.3 3.1 copy-start.2
  137.0 0.7 copy-start.14
  148.1 14.3 %all-to-all-start = ((s32[8,1,256]{2,1,0:T(1,128)}), s32[8,1,256]{2,1,0:T(1,128)S(1)}, u32[]{:S(2)}, u32[]{:S(2)}) async-start(s32[8,1,256]{2,1,0:T(1,128)} %bitcast.33), calls=%async_computation | async-start | bytes 16384 | tf_op jit(solution)/shard_map/all_to_all | solution.py:109
  162.4 85.6 %all-to-all-start.1 = ((bf16[8,256,256]{2,1,0:T(8,128)(2,1)}), bf16[8,256,256]{2,1,0:T(8,128)(2,1)S(1)}, u32[]{:S(2)}, u32[]{:S(2)}) async-start(bf16[8,256,256]{2,1,0:T(8,128)(2,1)} %bitcast.41), calls=%async_computation.1 | async-start | bytes 2097152 | tf_op jit(solution)/shard_map/all_to_all | solution.py:108
  315.1 2.4 copy-start.15
Sparse Core Ops, SparseCore 0:
  137.9 68.2 all-gather.7
where the time goes:
time: 326 us; the launch traced here: 324 us
  blocking collectives  113 us (35%)
  matrix products  83.5 us (26%)
  local copies, waits for them, and re-layouts  60.6 us (19%)
  other arithmetic  30.4 us (9%)
  starting transfers between devices  15.2 us (5%)
  between operations  14.5 us (4%)
  waiting for transfers between devices  6.34 us (2%)
    all_gather x5, blocking collectives, merged_2(): gathered = jax.tree.map(lambda a: lax.all_gather(a, axis), part)  113 us
    dot_general x8, matrix products, head_group(): jnp.einsum('hqk,khd->qhd', weights, value_rows, preferred_element_type=jn...  36.1 us
    sub x8, matrix products, head_group(): weights = jax.nn.softmax(scores, axis=-1).astype(jnp.bfloat16)  27 us
    unnamed x45, local copies, waits for them, and re-layouts  16.9 us
    dynamic_slice x26, local copies, waits for them, and re-layouts, take(): lax.dynamic_index_in_dim(a, source, 0, False)  11.3 us
    scatter x1, local copies, waits for them, and re-layouts, reorder(): placed.at[arrived_slots.reshape(-1)]  10.2 us
    add x10, other arithmetic, combine(): first_summed * first_factor[:, :, None]  7.23 us
  transfers between devices with their start and end apart: 5, of which 2 were waited for; matrix products, arithmetic and copies ran while one was open for 14% of the time, Pallas kernels for 0%

commit v1 on v0

v1 whole, which is shorter than its diff:
```python
import functools
import math

import jax
import jax.numpy as jnp
from jax import lax
from jax.experimental import pallas as pl
from jax.experimental.pallas import tpu as pltpu
from jax.sharding import PartitionSpec as P

C = 256
HEADS = 16
HDIM = 16
PATCH = 1024
DHEADS = 8
DHDIM = 32
BITS = 18
AUX = 16
STATS = 384
MESH = pl.DeviceIdType.MESH
F32 = jnp.float32
BF16 = jnp.bfloat16


def layer_norm(values):
    average = jnp.mean(values, axis=-1, keepdims=True)
    centered = values - average
    variance = jnp.mean(centered * centered, axis=-1, keepdims=True)
    return centered * lax.rsqrt(variance + 1e-05)


def dot(a, b):
    return jnp.dot(a, b, preferred_element_type=F32)


def dot_t(a, b):
    return lax.dot_general(a, b, (((1,), (1,)), ((), ())), preferred_element_type=F32)


def iota(shape, dim):
    return lax.broadcasted_iota(jnp.int32, shape, dim)


def block_kernel(
    devices,
    x_ref,
    prev_ref,
    next_ref,
    rank_ref,
    qkv_ref,
    proj_ref,
    up_ref,
    down_ref,
    norm_ref,
    out_ref,
    q_s,
    k_s,
    v_s,
    acc_s,
    blk_s,
):
    rows = x_ref.shape[0]
    half = rows // 2
    tile = 256
    ones = jnp.ones((half, 128), BF16)
    normed = layer_norm(x_ref[...].astype(F32)).astype(BF16)
    projected = dot(normed, qkv_ref[...]).astype(BF16)
    for side in range(2):
        own = projected[side * half : (side + 1) * half]
        other_rows = (prev_ref if side == 0 else next_ref)[...]
        other = dot(layer_norm(other_rows.astype(F32)).astype(BF16), qkv_ref[:, C:]).astype(BF16)
        q_s[side] = own[:, :C] * jnp.asarray(1.0 / math.sqrt(HDIM), BF16)
        k_s[side, :half] = own[:, C : 2 * C]
        k_s[side, half:] = other[:, :C]
        for group in range(2):
            lo = 2 * C + 128 * group
            v_s[side, group, :half, :128] = own[:, lo : lo + 128]
            v_s[side, group, :half, 128:] = ones
            v_s[side, group, half:, :128] = other[:, lo - C : lo - C + 128]
            v_s[side, group, half:, 128:] = ones
    acc_s[...] = jnp.zeros_like(acc_s)

    together = (iota((C, C), 0) // HDIM == iota((C, C), 1) // HDIM).astype(BF16)

    def most(ref):
        best = jnp.float32(0.0)
        for side in range(2):
            values = ref[side].astype(F32)
            best = jnp.maximum(best, jnp.max(dot((values * values).astype(BF16), together)))
        return best

    small = most(q_s) * most(k_s) <= 3600.0

    def heads(shifted):
        lane = iota((1, C), 1)

        def step(head, carry):
            for group in range(2):
                q_mask = (lane // HDIM == head + 8 * group).astype(F32).astype(BF16)
                v_mask = ((lane % 128) // HDIM == head).astype(F32).astype(BF16)
                for side in range(2):
                    q = q_s[side] * q_mask
                    total = acc_s[side, group]
                    if shifted:
                        top = jnp.max(dot_t(q, k_s[side]), axis=1, keepdims=True)
                    for start in range(0, 2 * half, tile):
                        scores = dot_t(q, k_s[side, start : start + tile])
                        if shifted:
                            scores = scores - top
                        weights = jnp.exp(scores).astype(BF16)
                        total = total + dot(weights, v_s[side, group, start : start + tile] * v_mask)
                    acc_s[side, group] = total
            return carry

        lax.fori_loop(0, 8, step, 0)

    @pl.when(small)
    def _():
        heads(False)

    @pl.when(jnp.logical_not(small))
    def _():
        heads(True)

    for side in range(2):
        part = slice(side * half, (side + 1) * half)
        attended = jnp.concatenate(
            [acc_s[side, group, :, :128] / acc_s[side, group, :, 128:] for group in range(2)], axis=1
        ).astype(BF16)
        middle = (x_ref[part].astype(F32) + dot(attended, proj_ref[...])).astype(BF16).astype(F32)
        normed_mid = layer_norm(middle).astype(BF16)
        hidden = jax.nn.gelu(dot(normed_mid, up_ref[...]), approximate=True).astype(BF16)
        block = (middle + dot(hidden, down_ref[...])).astype(BF16)
        blk_s[part] = block
        norm_ref[part] = layer_norm(block.astype(F32)).astype(BF16)

    capacity = 2 * rows // devices
    rank = rank_ref[...]
    target = rank // rows
    local = rank % rows
    high = (local // 256 + 1).astype(F32).astype(BF16)
    low = (local % 256).astype(F32).astype(BF16)
    aux_row = iota((AUX, rows), 0)
    aux = jnp.where(aux_row == 0, high.astype(F32), jnp.where(aux_row == 1, low.astype(F32), 0.0)).astype(BF16)
    goes = (iota((devices, rows), 0) == target).astype(F32)
    ahead = (iota((rows, rows), 0) < iota((rows, rows), 1)).astype(F32).astype(BF16)
    before = jnp.sum(goes * dot(goes.astype(BF16), ahead), axis=0, keepdims=True).astype(jnp.int32)
    block = blk_s[...]
    for t in range(devices):
        place = jnp.where(target == t, before, -1)
        chosen = (iota((C, rows), 0) == place).astype(F32).astype(BF16)
        out_ref[t, :capacity] = dot(chosen[:capacity], block).astype(BF16)
        out_ref[t, capacity:] = dot_t(aux, chosen).astype(BF16)


def decoder_kernel(queries_ref, dq_ref, dkv_ref, norm_ref, bits_ref, stats_ref):
    count = queries_ref.shape[0]
    rows = norm_ref.shape[0]
    key_value = dot(norm_ref[...], dkv_ref[...]).astype(BF16)
    query_heads = dot(queries_ref[...], dq_ref[...]).astype(BF16)
    pieces = []
    for start in range(0, count, 8):
        index = iota((8, rows), 0) + start
        first, last = start // BITS, (start + 7) // BITS
        word = bits_ref[first : first + 1, :]
        if last != first:
            word = jnp.where(index < last * BITS, word, bits_ref[last : last + 1, :])
        bit = jnp.right_shift(jnp.broadcast_to(word, (8, rows)), index % BITS) & 1
        pieces.append(jnp.where(bit == 1, 0.0, -1e30).astype(F32))
    bias = jnp.concatenate(pieces, axis=0)
    lane = iota((1, C), 1)
    slot = iota((count, 128), 1)
    stats = jnp.zeros((count, 128), F32)
    for group in range(2):
        total = jnp.zeros((count, C), F32)
        ones = jnp.ones((rows, 128), BF16)
        values = jnp.concatenate([key_value[:, C + 128 * group : C + 128 * (group + 1)], ones], axis=1)
        for inner in range(4):
            head = 4 * group + inner
            q_mask = (lane // DHDIM == head).astype(F32).astype(BF16)
            v_mask = ((lane % 128) // DHDIM == inner).astype(F32).astype(BF16)
            scores = dot_t(query_heads * q_mask, key_value[:, :C]) * (1.0 / math.sqrt(DHDIM)) + bias
            top = jnp.max(scores, axis=1, keepdims=True)
            weights = jnp.exp(scores - top).astype(BF16)
            total = total + dot(weights, values * v_mask)
            stats = jnp.where(slot == head, top, stats)
        for inner in range(4):
            head = 4 * group + inner
            column = 128 + DHDIM * inner
            stats = jnp.where(slot == DHEADS + head, total[:, column : column + 1], stats)
        stats_ref[:count, 128 * group : 128 * (group + 1)] = total[:, :128]
    stats_ref[:count, 2 * 128 :] = stats
    if stats_ref.shape[0] > count:
        rest = stats_ref.shape[0] - count
        stats_ref[count:, :256] = jnp.zeros((rest, 256), F32)
        stats_ref[count:, 256:] = jnp.where(iota((rest, 128), 1) < DHEADS, 0.0, 1.0).astype(F32)


def spread(columns):
    lane = iota((1, C), 1)
    wide = jnp.zeros((columns.shape[0], C), F32)
    for head in range(DHEADS):
        wide = jnp.where(lane // DHDIM == head, columns[:, head : head + 1], wide)
    return wide


def merge(parts):
    best = parts[0][:, C : C + DHEADS]
    for part in parts[1:]:
        best = jnp.maximum(best, part[:, C : C + DHEADS])
    summed, total = 0.0, 0.0
    for part in parts:
        factor = jnp.exp(part[:, C : C + DHEADS] - best)
        summed = summed + part[:, :C] * spread(factor)
        total = total + part[:, C + DHEADS : C + 2 * DHEADS] * factor
    return summed, total, best


def merge_kernel(
    scenes,
    seqs,
    stats_ref,
    queries_ref,
    out_w_ref,
    updated_ref,
    land_a,
    mid,
    land_b,
    result,
    send_a,
    recv_a,
    send_b,
    recv_b,
    send_c,
    recv_c,
    send_d,
    recv_d,
):
    scene, seq = lax.axis_index("scene"), lax.axis_index("seq")
    chunk = stats_ref.shape[0] // scenes
    piece = chunk // seqs

    def on_scene(offset):
        return lax.rem(scene + offset, scenes)

    def on_seq(offset):
        return lax.rem(seq + offset, seqs)

    barrier = pltpu.get_barrier_semaphore()
    for offset in range(1, scenes):
        pl.semaphore_signal(barrier, inc=1, device_id=(on_scene(offset), seq), device_id_type=MESH)
    for offset in range(1, seqs):
        pl.semaphore_signal(barrier, inc=1, device_id=(scene, on_seq(offset)), device_id_type=MESH)
    pl.semaphore_wait(barrier, scenes + seqs - 2)

    def send(source, dest, out_sem, in_sem, device):
        copy = pltpu.make_async_remote_copy(
            src_ref=source, dst_ref=dest, send_sem=out_sem, recv_sem=in_sem,
            device_id=device, device_id_type=MESH,
        )
        copy.start()
        return copy

    copies = []
    for offset in range(1, scenes):
        to = on_scene(offset)
        start = pl.multiple_of(to * chunk, 8)
        copies.append(send(stats_ref.at[pl.ds(start, chunk)], land_a.at[offset - 1],
                           send_a.at[offset - 1], recv_a.at[offset - 1], (to, seq)))
    for copy in copies:
        copy.wait()
    mine = stats_ref[pl.ds(pl.multiple_of(scene * chunk, 8), chunk), :]
    summed, total, best = merge([mine] + [land_a[i] for i in range(scenes - 1)])
    lane = iota((chunk, 128), 1)
    stats = jnp.zeros((chunk, 128), F32)
    for head in range(DHEADS):
        stats = jnp.where(lane == head, best[:, head : head + 1], stats)
        stats = jnp.where(lane == DHEADS + head, total[:, head : head + 1], stats)
    mid[:, :C] = summed
    mid[:, C:] = stats
    copies = []
    for offset in range(1, seqs):
        to = on_seq(offset)
        start = pl.multiple_of(to * piece, 8)
        copies.append(send(mid.at[pl.ds(start, piece)], land_b.at[offset - 1],
                           send_b.at[offset - 1], recv_b.at[offset - 1], (scene, to)))
    for copy in copies:
        copy.wait()
    mine = mid[pl.ds(pl.multiple_of(seq * piece, 8), piece), :]
    summed, total, best = merge([mine] + [land_b[i] for i in range(seqs - 1)])
    cross = (summed / spread(total)).astype(BF16)
    place = pl.multiple_of(scene * chunk + seq * piece, 8)
    rows = queries_ref[pl.ds(place, piece), :] + dot(cross, out_w_ref[...])
    result[pl.ds(place, piece), :] = layer_norm(rows)
    copies = []
    for offset in range(1, seqs):
        part = result.at[pl.ds(place, piece)]
        copies.append(send(part, part, send_c.at[offset - 1], recv_c.at[offset - 1], (scene, on_seq(offset))))
    for copy in copies:
        copy.wait()
    copies = []
    for offset in range(1, scenes):
        part = result.at[pl.ds(pl.multiple_of(scene * chunk, 8), chunk)]
        copies.append(send(part, part, send_d.at[offset - 1], recv_d.at[offset - 1], (on_scene(offset), seq)))
    for copy in copies:
        copy.wait()
    updated_ref[...] = result[...]


def logits_kernel(updated_ref, mask_ref, norm_ref, out_ref):
    embed = dot(updated_ref[...].astype(BF16), mask_ref[...]).astype(BF16)
    out_ref[...] = (dot_t(embed, norm_ref[...]) * (1.0 / math.sqrt(C))).astype(BF16)


def unpack_kernel(devices, in_ref, out_ref):
    rows = out_ref.shape[0]
    capacity = 2 * rows // devices
    total = jnp.zeros(out_ref.shape, F32)
    for t in range(devices):
        aux = in_ref[t, capacity:].astype(F32).astype(jnp.int32)
        slot = (aux[0:1] - 1) * 256 + aux[1:2]
        chosen = (iota((rows, C), 0) == slot).astype(F32).astype(BF16)
        total = total + dot(chosen[:, :capacity], in_ref[t, :capacity])
    out_ref[...] = total.astype(BF16)


def vmem(n):
    return [pl.BlockSpec(memory_space=pltpu.VMEM)] * n


def body(
    points,
    serial_rank,
    mask_bits,
    qkv_weight,
    proj_weight,
    up_weight,
    down_weight,
    queries,
    dec_q_weight,
    dec_kv_weight,
    dec_out_weight,
    mask_weight,
):
    rows = points.shape[0]
    half = rows // 2
    seqs, scenes = lax.axis_size("seq"), lax.axis_size("scene")
    capacity = 2 * rows // seqs
    count = queries.shape[0]
    params = pltpu.CompilerParams(vmem_limit_bytes=56 * 1024 * 1024)
    prev_half = lax.ppermute(points[half:], "seq", [(i, (i + 1) % seqs) for i in range(seqs)])
    next_half = lax.ppermute(points[:half], "seq", [((i + 1) % seqs, i) for i in range(seqs)])
    normed, outgoing = pl.pallas_call(
        functools.partial(block_kernel, seqs),
        out_shape=(
            jax.ShapeDtypeStruct((rows, C), BF16),
            jax.ShapeDtypeStruct((seqs, capacity + AUX, C), BF16),
        ),
        in_specs=vmem(8),
        out_specs=tuple(vmem(2)),
        scratch_shapes=[
            pltpu.VMEM((2, half, C), BF16),
            pltpu.VMEM((2, 2 * half, C), BF16),
            pltpu.VMEM((2, 2, 2 * half, C), BF16),
            pltpu.VMEM((2, 2, half, C), F32),
            pltpu.VMEM((rows, C), BF16),
        ],
        compiler_params=params,
        name="block",
    )(points, prev_half, next_half, serial_rank.reshape(1, rows), qkv_weight, proj_weight, up_weight, down_weight)
    arrived = lax.all_to_all(outgoing, "seq", split_axis=0, concat_axis=0, tiled=True)
    piece = -(-count // (8 * seqs * scenes)) * 8
    padded = piece * seqs * scenes
    stats = pl.pallas_call(
        decoder_kernel,
        out_shape=jax.ShapeDtypeStruct((padded, STATS), F32),
        in_specs=vmem(5),
        out_specs=vmem(1)[0],
        compiler_params=params,
        cost_estimate=pl.CostEstimate(flops=2 * 10**9, bytes_accessed=2 * 10**6, transcendentals=2 * 10**6),
        name="decode",
    )(queries, dec_q_weight, dec_kv_weight, normed, mask_bits)
    wide_queries = jnp.pad(queries.astype(F32), ((0, padded - count), (0, 0)))
    updated = pl.pallas_call(
        functools.partial(merge_kernel, scenes, seqs),
        out_shape=jax.ShapeDtypeStruct((padded, C), F32),
        in_specs=vmem(3),
        out_specs=vmem(1)[0],
        scratch_shapes=[
            pltpu.VMEM((scenes - 1, padded // scenes, STATS), F32),
            pltpu.VMEM((padded // scenes, STATS), F32),
            pltpu.VMEM((seqs - 1, piece, STATS), F32),
            pltpu.VMEM((padded, C), F32),
        ]
        + [pltpu.SemaphoreType.DMA((n - 1,)) for n in (scenes, scenes, seqs, seqs, seqs, seqs, scenes, scenes)],
        compiler_params=pltpu.CompilerParams(collective_id=0, has_side_effects=True),
        cost_estimate=pl.CostEstimate(flops=10**9, bytes_accessed=2 * 10**6, transcendentals=10**5),
        name="merge",
    )(stats, wide_queries, dec_out_weight)
    updated = updated[:count]
    logits = pl.pallas_call(
        logits_kernel,
        out_shape=jax.ShapeDtypeStruct((count, rows), BF16),
        in_specs=vmem(3),
        out_specs=vmem(1)[0],
        compiler_params=params,
        name="logits",
    )(updated, mask_weight, normed)
    reserialized = pl.pallas_call(
        functools.partial(unpack_kernel, seqs),
        out_shape=jax.ShapeDtypeStruct((rows, C), BF16),
        in_specs=vmem(1),
        out_specs=vmem(1)[0],
        compiler_params=params,
        name="unpack",
    )(arrived)
    return (reserialized, updated, logits)


def solution(mesh):
    split = ("scene", "seq")
    in_specs = (P(split, None), P(split), P(None, split)) + (P(),) * 9
    out_specs = (P(split, None), P(), P(None, split))
    return jax.shard_map(body, mesh=mesh, in_specs=in_specs, out_specs=out_specs, check_vma=False)
```

time: 326 us -> 111 us (0.34)
  blocking collectives: 113 us -> 0 us
  Pallas kernels: 0 us -> 84.1 us
  matrix products: 83.5 us -> 0 us
  local copies, waits for them, and re-layouts: 60.6 us -> 4.4 us
  other arithmetic: 30.4 us -> 0.74 us
  between operations: 14.5 us -> 0.65 us
  starting transfers between devices: 15.2 us -> 10.9 us
    all_gather x5 -> x0, blocking collectives: 113 us -> none  [merged_2(): gathered = jax.tree.map(lambda a: lax.all_gather(a, axis), part)]
    pallas_call x0 -> x5, Pallas kernels: none -> 84.1 us  [the longest x1 39.5 us: body(): pl.pallas_call(functools.partial(block_kernel, seqs), out_shape=(jax.Shap...]
    dot_general x19 -> x0, matrix products: 56.5 us -> none  [the longest x8 36.1 us: head_group(): jnp.einsum('hqk,khd->qhd', weights, value_rows, preferred_element_type=jn...]
    sub x8 -> x0, matrix products: 27 us -> none  [head_group(): weights = jax.nn.softmax(scores, axis=-1).astype(jnp.bfloat16)]
    unnamed x45 -> x8, local copies, waits for them, and re-layouts: 16.9 us -> 1.71 us
    dynamic_slice x38 -> x0, local copies, waits for them, and re-layouts: 13.7 us -> none  [the longest x26 11.3 us: take(): lax.dynamic_index_in_dim(a, source, 0, False)]
    scatter x1 -> x0, local copies, waits for them, and re-layouts: 10.2 us -> none  [reorder(): placed.at[arrived_slots.reshape(-1)]]
    add x22 -> x0, other arithmetic: 9.52 us -> none  [the longest x10 7.23 us: combine(): first_summed * first_factor[:, :, None]]
  transfers between devices with their start and end apart: 5 -> 3, of which waited for: 2 -> 2; matrix products, arithmetic and copies ran while one was open for 14% -> 2% of each run, Pallas kernels for 0% -> 38%
where the time goes in v1:
time: 111 us; the launch traced here: 110 us
  Pallas kernels  84.1 us (76%)
  starting transfers between devices  10.9 us (10%)
  waiting for transfers between devices  9.42 us (8%)
  local copies, waits for them, and re-layouts  4.4 us (4%)
    pallas_call x1, Pallas kernels, body(): pl.pallas_call(functools.partial(block_kernel, seqs), out_shape=(jax.Shap...  39.5 us
    pallas_call x1, Pallas kernels, body(): pl.pallas_call(functools.partial(merge_kernel, scenes, seqs), out_shape=j...  33.2 us
    ppermute x1, waiting for transfers between devices, body(): lax.ppermute(points[half:], 'seq', [(i, (i + 1) % seqs) for i in range(se...  7.5 us
    all_to_all x1, starting transfers between devices, body(): lax.all_to_all(outgoing, 'seq', split_axis=0, concat_axis=0, tiled=True)  5.73 us
    pallas_call x1, Pallas kernels, body(): pl.pallas_call(decoder_kernel, out_shape=jax.ShapeDtypeStruct((padded, ST...  5.72 us
    pallas_call x1, Pallas kernels, body(): pl.pallas_call(functools.partial(unpack_kernel, seqs), out_shape=jax.Shap...  3.28 us
    ppermute x1, starting transfers between devices, body(): lax.ppermute(points[:half], 'seq', [((i + 1) % seqs, i) for i in range(se...  3.1 us
    pallas_call x1, Pallas kernels, body(): pl.pallas_call(logits_kernel, out_shape=jax.ShapeDtypeStruct((count, rows...  2.4 us
  transfers between devices with their start and end apart: 3, of which 2 were waited for; matrix products, arithmetic and copies ran while one was open for 2% of the time, Pallas kernels for 38%

profile of v1, /device:TPU:1, one launch (start us, length us, event | category | flops | bytes accessed | tf_op | source)
XLA Modules:
  0.0 110.2 jit_solution(7946255442560494088)
XLA Ops:
  0.6 1.1 fusion
  1.7 2.1 %collective-permute-start = (bf16[512,256]{1,0:T(8,128)(2,1)S(1)}, bf16[512,256]{1,0:T(8,128)(2,1)S(1)}, u32[]{:S(2)}, u32[]{:S(2)}) collective-permute-start(bf16[512,256]{1,0:T(8,128)(2,1)S(1)} %get-tuple-element.8), channel_id=1, source_target_pairs={{0,1},{1,2},{2,3},{3,4},{4,5},{5,6},{6,7},{7,0},{8,9},{9,10},{10,1... | collective-permute-start | bytes 786440 | tf_op jit(solution)/shard_map/ppermute | solution.py:351
  3.8 3.1 %collective-permute-start.1 = (bf16[512,256]{1,0:T(8,128)(2,1)S(1)}, bf16[512,256]{1,0:T(8,128)(2,1)S(1)}, u32[]{:S(2)}, u32[]{:S(2)}) collective-permute-start(bf16[512,256]{1,0:T(8,128)(2,1)S(1)} %get-tuple-element.7), channel_id=1, source_target_pairs={{1,0},{2,1},{3,2},{4,3},{5,4},{6,5},{7,6},{0,7},{9,8},{10,9},{11,1... | collective-permute-start | bytes 786440 | tf_op jit(solution)/shard_map/ppermute | solution.py:352
  6.9 7.5 %collective-permute-done.prev_ref = bf16[512,256]{1,0:T(8,128)(2,1)S(1)} collective-permute-done((bf16[512,256]{1,0:T(8,128)(2,1)S(1)}, bf16[512,256]{1,0:T(8,128)(2,1)S(1)}, u32[]{:S(2)}, u32[]{:S(2)}) %collective-permute-start) | collective-permute-done | bytes 262176 | tf_op jit(solution)/shard_map/ppermute | solution.py:351
  14.4 0.0 copy-start.1
  14.4 1.9 %collective-permute-done.1.next_ref = bf16[512,256]{1,0:T(8,128)(2,1)S(1)} collective-permute-done((bf16[512,256]{1,0:T(8,128)(2,1)S(1)}, bf16[512,256]{1,0:T(8,128)(2,1)S(1)}, u32[]{:S(2)}, u32[]{:S(2)}) %collective-permute-start.1) | collective-permute-done | bytes 262176 | tf_op jit(solution)/shard_map/ppermute | solution.py:352
  16.3 0.0 copy-start.2
  16.3 0.0 copy-done.1
  16.3 0.7 copy-done.2
  17.0 39.5 %block.1 = (bf16[1024,256]{1,0:T(8,128)(2,1)}, bf16[8,272,256]{2,1,0:T(8,128)(2,1)}) custom-call(bf16[1024,256]{1,0:T(8,128)(2,1)} %x_ref.1, bf16[512,256]{1,0:T(8,128)(2,1)} %copy-done.1, bf16[512,256]{1,0:T(8,128)(2,1)} %copy-done.2, s32[1,1024]{1,0:T(1,128)} %bitcast.1, bf16[256,768]{1,0:T(8,128)(2,1)} %qkv_ref.1, bf16[256,256]{1,0:T(8,128)(2,1)} %proj_ref.1, ...), custom_call_target="tpu_custom_call" | custom-call | tf_op jit(solution)/shard_map/block/pallas_call | solution.py:353
  56.5 0.0 copy-start.3
  56.5 5.7 %all-to-all-start = ((bf16[8,272,256]{2,1,0:T(8,128)(2,1)}), bf16[8,272,256]{2,1,0:T(8,128)(2,1)S(1)}, u32[]{:S(2)}, u32[]{:S(2)}) async-start(bf16[8,272,256]{2,1,0:T(8,128)(2,1)} %get-tuple-element.5), calls=%async_computation | async-start | bytes 2228224 | tf_op jit(solution)/shard_map/all_to_all | solution.py:371
  62.2 0.0 copy-done.3
  62.2 0.7 pad_convert_fusion.queries_ref
  63.0 5.7 %decode.1.stats_ref = f32[256,384]{1,0:T(8,128)} custom-call(bf16[200,256]{1,0:T(8,128)(2,1)} %queries_ref.1, bf16[256,256]{1,0:T(8,128)(2,1)} %dq_ref.1, bf16[256,512]{1,0:T(8,128)(2,1)} %dkv_ref.1, bf16[1024,256]{1,0:T(8,128)(2,1)} %get-tuple-element.6.norm_ref, s32[12,1024]{1,0:T(8,128)} %bits_ref.1), custom_call_target="tpu_custom_call" | custom-call | flops 2000000000 | bytes 2000000 | tf_op jit(solution)/shard_map/decode/pallas_call | solution.py:374
  68.7 33.2 %merge.1 = f32[256,256]{1,0:T(8,128)} custom-call(f32[256,384]{1,0:T(8,128)} %decode.1.stats_ref, f32[256,256]{1,0:T(8,128)} %pad_convert_fusion.queries_ref, bf16[256,256]{1,0:T(8,128)(2,1)} %out_w_ref.1), custom_call_target="tpu_custom_call" | custom-call | flops 1000000000 | bytes 2000000 | tf_op jit(solution)/shard_map/merge/pallas_call | solution.py:384
  101.9 1.6 %slice.11.updated_ref = f32[200,256]{1,0:T(8,128)} slice(f32[256,256]{1,0:T(8,128)} %merge.1), slice={[0:200], [0:256]} | slice | bytes 409600 | tf_op jit(solution)/shard_map/slice | solution.py:400
  103.5 2.4 %logits.1 = bf16[200,1024]{1,0:T(8,128)(2,1)} custom-call(f32[200,256]{1,0:T(8,128)} %slice.11.updated_ref, bf16[256,256]{1,0:T(8,128)(2,1)} %mask_ref.1, bf16[1024,256]{1,0:T(8,128)(2,1)} %get-tuple-element.6.norm_ref), custom_call_target="tpu_custom_call" | custom-call | tf_op jit(solution)/shard_map/logits/pallas_call | solution.py:401
  105.9 0.0 all-to-all-done.in_ref
  105.9 0.0 copy-start
  105.9 1.0 copy-done
  106.9 3.3 %unpack.1 = bf16[1024,256]{1,0:T(8,128)(2,1)} custom-call(bf16[8,272,256]{2,1,0:T(8,128)(2,1)} %copy-done), custom_call_target="tpu_custom_call" | custom-call | tf_op jit(solution)/shard_map/unpack/pallas_call | solution.py:409
Async XLA Ops:
  1.7 12.7 %collective-permute-start = (bf16[512,256]{1,0:T(8,128)(2,1)S(1)}, bf16[512,256]{1,0:T(8,128)(2,1)S(1)}, u32[]{:S(2)}, u32[]{:S(2)}) collective-permute-start(bf16[512,256]{1,0:T(8,128)(2,1)S(1)} %get-tuple-element.8), channel_id=1, source_target_pairs={{0,1},{1,2},{2,3},{3,4},{4,5},{5,6},{6,7},{7,0},{8,9},{9,10},{10,1... | collective-permute-start | bytes 786440 | tf_op jit(solution)/shard_map/ppermute | solution.py:351
  3.8 12.5 %collective-permute-start.1 = (bf16[512,256]{1,0:T(8,128)(2,1)S(1)}, bf16[512,256]{1,0:T(8,128)(2,1)S(1)}, u32[]{:S(2)}, u32[]{:S(2)}) collective-permute-start(bf16[512,256]{1,0:T(8,128)(2,1)S(1)} %get-tuple-element.7), channel_id=1, source_target_pairs={{1,0},{2,1},{3,2},{4,3},{5,4},{6,5},{7,6},{0,7},{9,8},{10,9},{11,1... | collective-permute-start | bytes 786440 | tf_op jit(solution)/shard_map/ppermute | solution.py:352
  14.4 1.9 %copy-start.1 = (bf16[512,256]{1,0:T(8,128)(2,1)}, bf16[512,256]{1,0:T(8,128)(2,1)S(1)}, u32[]{:S(2)}) copy-start(bf16[512,256]{1,0:T(8,128)(2,1)S(1)} %collective-permute-done.prev_ref) | copy-start | bytes 786436
  16.3 0.7 copy-start.2
  56.5 5.7 %copy-start.3 = (bf16[200,256]{1,0:T(8,128)(2,1)S(1)}, bf16[200,256]{1,0:T(8,128)(2,1)}, u32[]{:S(2)}) copy-start(bf16[200,256]{1,0:T(8,128)(2,1)} %queries_ref.1) | copy-start | bytes 307204
  56.5 49.4 %all-to-all-start = ((bf16[8,272,256]{2,1,0:T(8,128)(2,1)}), bf16[8,272,256]{2,1,0:T(8,128)(2,1)S(1)}, u32[]{:S(2)}, u32[]{:S(2)}) async-start(bf16[8,272,256]{2,1,0:T(8,128)(2,1)} %get-tuple-element.5), calls=%async_computation | async-start | bytes 2228224 | tf_op jit(solution)/shard_map/all_to_all | solution.py:371
  105.9 1.0 copy-start

commit v2 on v1

--- a/solution.py
+++ b/solution.py
@@ -216,13 +216,31 @@
     return summed, total, best
 
 
-def merge_kernel(
+def unpack(piece, rows, capacity):
+    aux = piece[capacity:].astype(F32).astype(jnp.int32)
+    slot = (aux[0:1] - 1) * 256 + aux[1:2]
+    chosen = (iota((rows, C), 0) == slot).astype(F32).astype(BF16)
+    return dot(chosen[:, :capacity], piece[:capacity])
+
+
+def tail_kernel(
     scenes,
     seqs,
+    outgoing_ref,
+    norm_ref,
+    bits_ref,
+    queries_ref,
+    dq_ref,
+    dkv_ref,
+    out_w_ref,
+    mask_ref,
+    reserialized_ref,
+    updated_ref,
+    logits_ref,
     stats_ref,
-    queries_ref,
-    out_w_ref,
-    updated_ref,
+    wide_ref,
+    arrived,
+    placed,
     land_a,
     mid,
     land_b,
@@ -235,8 +253,13 @@
     recv_c,
     send_d,
     recv_d,
+    send_e,
+    recv_e,
 ):
     scene, seq = lax.axis_index("scene"), lax.axis_index("seq")
+    count = queries_ref.shape[0]
+    rows = norm_ref.shape[0]
+    capacity = 2 * rows // seqs
     chunk = stats_ref.shape[0] // scenes
     piece = chunk // seqs
 
@@ -261,12 +284,29 @@
         copy.start()
         return copy
 
+    order = sorted(range(1, seqs), key=lambda offset: (abs(offset - seqs // 2), offset))
+    first, second = len(order) * 4 // 7, len(order) * 6 // 7
+    points = []
+
+    def send_points(offsets):
+        for offset in offsets:
+            to = on_seq(offset)
+            copy = send(outgoing_ref.at[to], arrived.at[offset - 1],
+                        send_e.at[offset - 1], recv_e.at[offset - 1], (scene, to))
+            points.append((offset, copy))
+
+    send_points(order[:first])
+    decoder_kernel(queries_ref, dq_ref, dkv_ref, norm_ref, bits_ref, stats_ref)
+    wide_ref[:count] = queries_ref[...].astype(F32)
+    if wide_ref.shape[0] > count:
+        wide_ref[count:] = jnp.zeros((wide_ref.shape[0] - count, C), F32)
     copies = []
     for offset in range(1, scenes):
         to = on_scene(offset)
         start = pl.multiple_of(to * chunk, 8)
         copies.append(send(stats_ref.at[pl.ds(start, chunk)], land_a.at[offset - 1],
                            send_a.at[offset - 1], recv_a.at[offset - 1], (to, seq)))
+    placed[...] = unpack(outgoing_ref[seq], rows, capacity)
     for copy in copies:
         copy.wait()
     mine = stats_ref[pl.ds(pl.multiple_of(scene * chunk, 8), chunk), :]
@@ -284,44 +324,40 @@
         start = pl.multiple_of(to * piece, 8)
         copies.append(send(mid.at[pl.ds(start, piece)], land_b.at[offset - 1],
                            send_b.at[offset - 1], recv_b.at[offset - 1], (scene, to)))
+    send_points(order[first:second])
     for copy in copies:
         copy.wait()
     mine = mid[pl.ds(pl.multiple_of(seq * piece, 8), piece), :]
     summed, total, best = merge([mine] + [land_b[i] for i in range(seqs - 1)])
     cross = (summed / spread(total)).astype(BF16)
     place = pl.multiple_of(scene * chunk + seq * piece, 8)
-    rows = queries_ref[pl.ds(place, piece), :] + dot(cross, out_w_ref[...])
-    result[pl.ds(place, piece), :] = layer_norm(rows)
+    result[pl.ds(place, piece), :] = layer_norm(wide_ref[pl.ds(place, piece), :] + dot(cross, out_w_ref[...]))
     copies = []
     for offset in range(1, seqs):
         part = result.at[pl.ds(place, piece)]
         copies.append(send(part, part, send_c.at[offset - 1], recv_c.at[offset - 1], (scene, on_seq(offset))))
+    send_points(order[second:])
     for copy in copies:
         copy.wait()
     copies = []
     for offset in range(1, scenes):
         part = result.at[pl.ds(pl.multiple_of(scene * chunk, 8), chunk)]
         copies.append(send(part, part, send_d.at[offset - 1], recv_d.at[offset - 1], (on_scene(offset), seq)))
+    for offset, copy in points[:first]:
+        copy.wait()
+        placed[...] += unpack(arrived[offset - 1], rows, capacity)
     for copy in copies:
         copy.wait()
-    updated_ref[...] = result[...]
-
-
-def logits_kernel(updated_ref, mask_ref, norm_ref, out_ref):
-    embed = dot(updated_ref[...].astype(BF16), mask_ref[...]).astype(BF16)
-    out_ref[...] = (dot_t(embed, norm_ref[...]) * (1.0 / math.sqrt(C))).astype(BF16)
-
-
-def unpack_kernel(devices, in_ref, out_ref):
-    rows = out_ref.shape[0]
-    capacity = 2 * rows // devices
-    total = jnp.zeros(out_ref.shape, F32)
-    for t in range(devices):
-        aux = in_ref[t, capacity:].astype(F32).astype(jnp.int32)
-        slot = (aux[0:1] - 1) * 256 + aux[1:2]
-        chosen = (iota((rows, C), 0) == slot).astype(F32).astype(BF16)
-        total = total + dot(chosen[:, :capacity], in_ref[t, :capacity])
-    out_ref[...] = total.astype(BF16)
+    updated = result[:count]
+    updated_ref[...] = updated
+    embed = dot(updated.astype(BF16), mask_ref[...]).astype(BF16)
+    logits_ref[...] = (dot_t(embed, norm_ref[...]) * (1.0 / math.sqrt(C))).astype(BF16)
+    for offset, copy in points[first:-1]:
+        copy.wait()
+        placed[...] += unpack(arrived[offset - 1], rows, capacity)
+    offset, copy = points[-1]
+    copy.wait()
+    reserialized_ref[...] = (placed[...] + unpack(arrived[offset - 1], rows, capacity)).astype(BF16)
 
 
 def vmem(n):
@@ -368,53 +404,36 @@
         compiler_params=params,
         name="block",
     )(points, prev_half, next_half, serial_rank.reshape(1, rows), qkv_weight, proj_weight, up_weight, down_weight)
-    arrived = lax.all_to_all(outgoing, "seq", split_axis=0, concat_axis=0, tiled=True)
     piece = -(-count // (8 * seqs * scenes)) * 8
     padded = piece * seqs * scenes
-    stats = pl.pallas_call(
-        decoder_kernel,
-        out_shape=jax.ShapeDtypeStruct((padded, STATS), F32),
-        in_specs=vmem(5),
-        out_specs=vmem(1)[0],
-        compiler_params=params,
-        cost_estimate=pl.CostEstimate(flops=2 * 10**9, bytes_accessed=2 * 10**6, transcendentals=2 * 10**6),
-        name="decode",
-    )(queries, dec_q_weight, dec_kv_weight, normed, mask_bits)
-    wide_queries = jnp.pad(queries.astype(F32), ((0, padded - count), (0, 0)))
-    updated = pl.pallas_call(
-        functools.partial(merge_kernel, scenes, seqs),
-        out_shape=jax.ShapeDtypeStruct((padded, C), F32),
-        in_specs=vmem(3),
-        out_specs=vmem(1)[0],
+    return pl.pallas_call(
+        functools.partial(tail_kernel, scenes, seqs),
+        out_shape=(
+            jax.ShapeDtypeStruct((rows, C), BF16),
+            jax.ShapeDtypeStruct((count, C), F32),
+            jax.ShapeDtypeStruct((count, rows), BF16),
+        ),
+        in_specs=vmem(8),
+        out_specs=tuple(vmem(3)),
         scratch_shapes=[
+            pltpu.VMEM((padded, STATS), F32),
+            pltpu.VMEM((padded, C), F32),
+            pltpu.VMEM((seqs - 1, capacity + AUX, C), BF16),
+            pltpu.VMEM((rows, C), F32),
             pltpu.VMEM((scenes - 1, padded // scenes, STATS), F32),
             pltpu.VMEM((padded // scenes, STATS), F32),
             pltpu.VMEM((seqs - 1, piece, STATS), F32),
             pltpu.VMEM((padded, C), F32),
         ]
-        + [pltpu.SemaphoreType.DMA((n - 1,)) for n in (scenes, scenes, seqs, seqs, seqs, seqs, scenes, scenes)],
-        compiler_params=pltpu.CompilerParams(collective_id=0, has_side_effects=True),
-        cost_estimate=pl.CostEstimate(flops=10**9, bytes_accessed=2 * 10**6, transcendentals=10**5),
-        name="merge",
-    )(stats, wide_queries, dec_out_weight)
-    updated = updated[:count]
-    logits = pl.pallas_call(
-        logits_kernel,
-        out_shape=jax.ShapeDtypeStruct((count, rows), BF16),
-        in_specs=vmem(3),
-        out_specs=vmem(1)[0],
-        compiler_params=params,
-        name="logits",
-    )(updated, mask_weight, normed)
-    reserialized = pl.pallas_call(
-        functools.partial(unpack_kernel, seqs),
-        out_shape=jax.ShapeDtypeStruct((rows, C), BF16),
-        in_specs=vmem(1),
-        out_specs=vmem(1)[0],
-        compiler_params=params,
-        name="unpack",
-    )(arrived)
-    return (reserialized, updated, logits)
+        + [
+            pltpu.SemaphoreType.DMA((n - 1,))
+            for n in (scenes, scenes, seqs, seqs, seqs, seqs, scenes, scenes, seqs, seqs)
+        ],
+        compiler_params=pltpu.CompilerParams(
+            collective_id=0, has_side_effects=True, vmem_limit_bytes=56 * 1024 * 1024
+        ),
+        name="tail",
+    )(outgoing, normed, mask_bits, queries, dec_q_weight, dec_kv_weight, dec_out_weight, mask_weight)
 
 
 def solution(mesh):

time: 111 us -> 102 us (0.919)
  starting transfers between devices: 10.9 us -> 5.12 us
  Pallas kernels: 84.1 us -> 81.5 us
    all_to_all x1 -> x0, starting transfers between devices: 5.73 us -> none  [body(): lax.all_to_all(outgoing, 'seq', split_axis=0, concat_axis=0, tiled=True)]
    ppermute x1, waiting for transfers between devices: 1.92 us -> 4.99 us  [body(): lax.ppermute(points[:half], 'seq', [((i + 1) % seqs, i) for i in range(se...]
    ppermute x1, waiting for transfers between devices: 7.5 us -> 4.62 us  [body(): lax.ppermute(points[half:], 'seq', [(i, (i + 1) % seqs) for i in range(se...]
    pallas_call x4 -> x1, Pallas kernels: 44.6 us -> 42.1 us  [body(): pl.pallas_call(functools.partial(tail_kernel, scenes, seqs), out_shape=(j...]
    unnamed x8 -> x11, local copies, waits for them, and re-layouts: 1.71 us -> 4.07 us
    ppermute x1, starting transfers between devices: 2.08 us -> 0.01 us  [body(): lax.ppermute(points[half:], 'seq', [(i, (i + 1) % seqs) for i in range(se...]
    ppermute x1, starting transfers between devices: 3.1 us -> 5.12 us  [body(): lax.ppermute(points[:half], 'seq', [((i + 1) % seqs, i) for i in range(se...]
    slice x1 -> x0, local copies, waits for them, and re-layouts: 1.62 us -> none  [body(): updated = updated[:count]]
  transfers between devices with their start and end apart: 3 -> 2, of which waited for: 2 -> 2; matrix products, arithmetic and copies ran while one was open for 2% -> 0% of each run, Pallas kernels for 38% -> 0%
where the time goes in v2:
time: 102 us
  Pallas kernels  81.5 us (80%)
  waiting for transfers between devices  9.6 us (9%)
  local copies, waits for them, and re-layouts  5.14 us (5%)
  starting transfers between devices  5.12 us (5%)
    pallas_call x1, Pallas kernels, body(): pl.pallas_call(functools.partial(tail_kernel, scenes, seqs), out_shape=(j...  42.1 us
    pallas_call x1, Pallas kernels, body(): pl.pallas_call(functools.partial(block_kernel, seqs), out_shape=(jax.Shap...  39.5 us
    ppermute x1, starting transfers between devices, body(): lax.ppermute(points[:half], 'seq', [((i + 1) % seqs, i) for i in range(se...  5.12 us
    ppermute x1, waiting for transfers between devices, body(): lax.ppermute(points[:half], 'seq', [((i + 1) % seqs, i) for i in range(se...  4.99 us
    ppermute x1, waiting for transfers between devices, body(): lax.ppermute(points[half:], 'seq', [(i, (i + 1) % seqs) for i in range(se...  4.62 us
    unnamed x11, local copies, waits for them, and re-layouts  4.07 us
  transfers between devices with their start and end apart: 2, of which 2 were waited for; matrix products, arithmetic and copies ran while one was open for 0% of the time, Pallas kernels for 0%

profile of v2, /device:TPU:1, one launch (start us, length us, event | category | flops | bytes accessed | tf_op | source)
XLA Modules:
  0.0 102.1 jit_solution(2662330162140557576)
XLA Ops:
  0.6 1.1 %fusion = (bf16[512,256]{1,0:T(8,128)(2,1)S(1)}, bf16[512,256]{1,0:T(8,128)(2,1)S(1)}) fusion(bf16[1024,256]{1,0:T(8,128)(2,1)} %x_ref.1), kind=kLoop, calls=%fused_computation | loop fusion | bytes 1048576 | tf_op jit(solution)/shard_map/slice | solution.py:388
  1.7 5.1 %collective-permute-start.1 = (bf16[512,256]{1,0:T(8,128)(2,1)S(1)}, bf16[512,256]{1,0:T(8,128)(2,1)S(1)}, u32[]{:S(2)}, u32[]{:S(2)}) collective-permute-start(bf16[512,256]{1,0:T(8,128)(2,1)S(1)} %get-tuple-element.7), channel_id=1, source_target_pairs={{1,0},{2,1},{3,2},{4,3},{5,4},{6,5},{7,6},{0,7},{9,8},{10,9},{11,1... | collective-permute-start | bytes 786440 | tf_op jit(solution)/shard_map/ppermute | solution.py:388
  6.8 0.0 collective-permute-start
  6.8 5.0 %collective-permute-done.1.next_ref = bf16[512,256]{1,0:T(8,128)(2,1)S(1)} collective-permute-done((bf16[512,256]{1,0:T(8,128)(2,1)S(1)}, bf16[512,256]{1,0:T(8,128)(2,1)S(1)}, u32[]{:S(2)}, u32[]{:S(2)}) %collective-permute-start.1) | collective-permute-done | bytes 262176 | tf_op jit(solution)/shard_map/ppermute | solution.py:388
  11.8 0.0 copy-start.1
  11.8 4.6 %collective-permute-done.prev_ref = bf16[512,256]{1,0:T(8,128)(2,1)S(1)} collective-permute-done((bf16[512,256]{1,0:T(8,128)(2,1)S(1)}, bf16[512,256]{1,0:T(8,128)(2,1)S(1)}, u32[]{:S(2)}, u32[]{:S(2)}) %collective-permute-start) | collective-permute-done | bytes 262176 | tf_op jit(solution)/shard_map/ppermute | solution.py:387
  16.4 0.0 copy-start.2
  16.4 0.0 copy-done.1
  16.4 0.7 copy-done.2
  17.1 39.5 %block.1 = (bf16[1024,256]{1,0:T(8,128)(2,1)}, bf16[8,272,256]{2,1,0:T(8,128)(2,1)}) custom-call(bf16[1024,256]{1,0:T(8,128)(2,1)} %x_ref.1, bf16[512,256]{1,0:T(8,128)(2,1)} %copy-done.2, bf16[512,256]{1,0:T(8,128)(2,1)} %copy-done.1, s32[1,1024]{1,0:T(1,128)} %bitcast.1, bf16[256,768]{1,0:T(8,128)(2,1)} %qkv_ref.1, bf16[256,256]{1,0:T(8,128)(2,1)} %proj_ref.1, ...), custom_call_target="tpu_custom_call" | custom-call | tf_op jit(solution)/shard_map/block/pallas_call | solution.py:389
  56.6 42.1 %tail.1 = (bf16[1024,256]{1,0:T(8,128)(2,1)}, f32[200,256]{1,0:T(8,128)}, bf16[200,1024]{1,0:T(8,128)(2,1)}) custom-call(bf16[8,272,256]{2,1,0:T(8,128)(2,1)} %get-tuple-element.5.outgoing_ref, bf16[1024,256]{1,0:T(8,128)(2,1)} %get-tuple-element.6.norm_ref, s32[12,1024]{1,0:T(8,128)} %bits_ref.1, bf16[200,256]{1,0:T(8,128)(2,1)} %queries_ref.1, ...), custom_call_target="tpu_custom_call" | custom-call | tf_op jit(solution)/shard_map/tail/pallas_call | solution.py:409
  98.7 0.0 copy-start.3
  98.7 0.0 copy-start
  98.7 1.9 %copy.18 = bf16[1024,256]{1,0:T(8,128)(2,1)} copy(bf16[1024,256]{1,0:T(8,128)(2,1)} %get-tuple-element.12) | data formatting | bytes 1048576
  100.6 0.0 copy-done.3
  100.6 0.7 copy.19
  101.3 0.0 copy-done
  101.3 0.8 copy.20
Async XLA Ops:
  1.7 10.1 %collective-permute-start.1 = (bf16[512,256]{1,0:T(8,128)(2,1)S(1)}, bf16[512,256]{1,0:T(8,128)(2,1)S(1)}, u32[]{:S(2)}, u32[]{:S(2)}) collective-permute-start(bf16[512,256]{1,0:T(8,128)(2,1)S(1)} %get-tuple-element.7), channel_id=1, source_target_pairs={{1,0},{2,1},{3,2},{4,3},{5,4},{6,5},{7,6},{0,7},{9,8},{10,9},{11,1... | collective-permute-start | bytes 786440 | tf_op jit(solution)/shard_map/ppermute | solution.py:388
  6.8 9.6 %collective-permute-start = (bf16[512,256]{1,0:T(8,128)(2,1)S(1)}, bf16[512,256]{1,0:T(8,128)(2,1)S(1)}, u32[]{:S(2)}, u32[]{:S(2)}) collective-permute-start(bf16[512,256]{1,0:T(8,128)(2,1)S(1)} %get-tuple-element.8), channel_id=1, source_target_pairs={{0,1},{1,2},{2,3},{3,4},{4,5},{5,6},{6,7},{7,0},{8,9},{9,10},{10,1... | collective-permute-start | bytes 786440 | tf_op jit(solution)/shard_map/ppermute | solution.py:387
  11.8 4.6 %copy-start.1 = (bf16[512,256]{1,0:T(8,128)(2,1)}, bf16[512,256]{1,0:T(8,128)(2,1)S(1)}, u32[]{:S(2)}) copy-start(bf16[512,256]{1,0:T(8,128)(2,1)S(1)} %collective-permute-done.1.next_ref) | copy-start | bytes 786436
  16.4 0.7 copy-start.2
  98.7 2.0 %copy-start.3 = (f32[200,256]{1,0:T(8,128)S(1)}, f32[200,256]{1,0:T(8,128)}, u32[]{:S(2)}) copy-start(f32[200,256]{1,0:T(8,128)} %get-tuple-element.13) | copy-start | bytes 614404
  98.7 2.6 %copy-start = (bf16[200,1024]{1,0:T(8,128)(2,1)S(1)}, bf16[200,1024]{1,0:T(8,128)(2,1)}, u32[]{:S(2)}) copy-start(bf16[200,1024]{1,0:T(8,128)(2,1)} %get-tuple-element.14) | copy-start | bytes 1228804

commit v3 on v2

--- a/solution.py
+++ b/solution.py
@@ -41,6 +41,83 @@
     return lax.broadcasted_iota(jnp.int32, shape, dim)
 
 
+def group_masks(head, group):
+    lane = iota((1, C), 1)
+    q_mask = (lane // HDIM == head + 8 * group).astype(F32).astype(BF16)
+    v_mask = ((lane % 128) // HDIM == head).astype(F32)
+    return q_mask, v_mask
+
+
+def fill(side, key_value, k_s, v_s):
+    k_s[side] = key_value[:, :C]
+    for group in range(2):
+        v_s[side, group, :, :128] = key_value[:, C + 128 * group : C + 128 * (group + 1)]
+        v_s[side, group, :, 128:] = jnp.ones((key_value.shape[0], 128), BF16)
+
+
+def most(ref):
+    together = (iota((C, C), 0) // HDIM == iota((C, C), 1) // HDIM).astype(BF16)
+    best = jnp.float32(0.0)
+    for side in range(2):
+        values = ref[side].astype(F32)
+        best = jnp.maximum(best, jnp.max(dot((values * values).astype(BF16), together)))
+    return best
+
+
+def attend(q_ref, k_s, v_s, acc_s, shift):
+    keys = k_s.shape[1]
+    tile = 256
+
+    def step(head, carry):
+        for group in range(2):
+            q_mask, v_mask = group_masks(head, group)
+            v_mask = v_mask.astype(BF16)
+            for side in range(2):
+                q = q_ref[side] * q_mask
+                total = acc_s[side, group]
+                if shift is not None:
+                    top = shift(side, group, head, jnp.max(dot_t(q, k_s[side]), axis=1, keepdims=True))
+                for start in range(0, keys, tile):
+                    scores = dot_t(q, k_s[side, start : start + tile])
+                    if shift is not None:
+                        scores = scores - top
+                    weights = jnp.exp(scores).astype(BF16)
+                    total = total + dot(weights, v_s[side, group, start : start + tile] * v_mask)
+                acc_s[side, group] = total
+        return carry
+
+    lax.fori_loop(0, 8, step, 0)
+
+
+def own_kernel(x_ref, qkv_ref, q_ref, acc_ref, top_ref, flag_ref, k_s, v_s):
+    half = x_ref.shape[0] // 2
+    normed = layer_norm(x_ref[...].astype(F32)).astype(BF16)
+    projected = dot(normed, qkv_ref[...]).astype(BF16)
+    for side in range(2):
+        own = projected[side * half : (side + 1) * half]
+        q_ref[side] = own[:, :C] * jnp.asarray(1.0 / math.sqrt(HDIM), BF16)
+        fill(side, own[:, C:], k_s, v_s)
+    acc_ref[...] = jnp.zeros_like(acc_ref)
+    top_ref[...] = jnp.zeros_like(top_ref)
+    most_q = most(q_ref)
+    small = most_q * most(k_s) <= 3600.0
+    flag_ref[0] = most_q
+    flag_ref[1] = jnp.where(small, 1.0, 0.0)
+
+    def shift(side, group, head, peak):
+        lane = iota((1, 128), 1)
+        top_ref[side] = jnp.where(lane == head + 8 * group, peak, top_ref[side])
+        return peak
+
+    @pl.when(small)
+    def _():
+        attend(q_ref, k_s, v_s, acc_ref, None)
+
+    @pl.when(jnp.logical_not(small))
+    def _():
+        attend(q_ref, k_s, v_s, acc_ref, shift)
+
+
 def block_kernel(
     devices,
     x_ref,
@@ -51,76 +128,44 @@
     proj_ref,
     up_ref,
     down_ref,
+    q_ref,
+    old_ref,
+    top_ref,
+    flag_ref,
     norm_ref,
     out_ref,
-    q_s,
     k_s,
     v_s,
     acc_s,
+    scale_s,
     blk_s,
 ):
     rows = x_ref.shape[0]
     half = rows // 2
-    tile = 256
-    ones = jnp.ones((half, 128), BF16)
-    normed = layer_norm(x_ref[...].astype(F32)).astype(BF16)
-    projected = dot(normed, qkv_ref[...]).astype(BF16)
     for side in range(2):
-        own = projected[side * half : (side + 1) * half]
         other_rows = (prev_ref if side == 0 else next_ref)[...]
         other = dot(layer_norm(other_rows.astype(F32)).astype(BF16), qkv_ref[:, C:]).astype(BF16)
-        q_s[side] = own[:, :C] * jnp.asarray(1.0 / math.sqrt(HDIM), BF16)
-        k_s[side, :half] = own[:, C : 2 * C]
-        k_s[side, half:] = other[:, :C]
-        for group in range(2):
-            lo = 2 * C + 128 * group
-            v_s[side, group, :half, :128] = own[:, lo : lo + 128]
-            v_s[side, group, :half, 128:] = ones
-            v_s[side, group, half:, :128] = other[:, lo - C : lo - C + 128]
-            v_s[side, group, half:, 128:] = ones
-    acc_s[...] = jnp.zeros_like(acc_s)
-
-    together = (iota((C, C), 0) // HDIM == iota((C, C), 1) // HDIM).astype(BF16)
-
-    def most(ref):
-        best = jnp.float32(0.0)
-        for side in range(2):
-            values = ref[side].astype(F32)
-            best = jnp.maximum(best, jnp.max(dot((values * values).astype(BF16), together)))
-        return best
-
-    small = most(q_s) * most(k_s) <= 3600.0
-
-    def heads(shifted):
-        lane = iota((1, C), 1)
-
-        def step(head, carry):
-            for group in range(2):
-                q_mask = (lane // HDIM == head + 8 * group).astype(F32).astype(BF16)
-                v_mask = ((lane % 128) // HDIM == head).astype(F32).astype(BF16)
-                for side in range(2):
-                    q = q_s[side] * q_mask
-                    total = acc_s[side, group]
-                    if shifted:
-                        top = jnp.max(dot_t(q, k_s[side]), axis=1, keepdims=True)
-                    for start in range(0, 2 * half, tile):
-                        scores = dot_t(q, k_s[side, start : start + tile])
-                        if shifted:
-                            scores = scores - top
-                        weights = jnp.exp(scores).astype(BF16)
-                        total = total + dot(weights, v_s[side, group, start : start + tile] * v_mask)
-                    acc_s[side, group] = total
-            return carry
-
-        lax.fori_loop(0, 8, step, 0)
+        fill(side, other, k_s, v_s)
+    small = jnp.logical_and(flag_ref[0] * most(k_s) <= 3600.0, flag_ref[1] > 0.5)
+
+    def shift(side, group, head, peak):
+        lane = iota((1, 128), 1)
+        old = jnp.max(jnp.where(lane == head + 8 * group, top_ref[side], -jnp.inf), axis=1, keepdims=True)
+        top = jnp.maximum(old, peak)
+        mask = group_masks(head, group)[1]
+        scale_s[side, group] = jnp.where(mask > 0.5, jnp.exp(old - top), scale_s[side, group])
+        return top
 
     @pl.when(small)
     def _():
-        heads(False)
+        acc_s[...] = old_ref[...]
+        attend(q_ref, k_s, v_s, acc_s, None)
 
     @pl.when(jnp.logical_not(small))
     def _():
-        heads(True)
+        acc_s[...] = jnp.zeros_like(acc_s)
+        attend(q_ref, k_s, v_s, acc_s, shift)
+        acc_s[...] = acc_s[...] + old_ref[...] * scale_s[...]
 
     for side in range(2):
         part = slice(side * half, (side + 1) * half)
@@ -383,27 +428,45 @@
     seqs, scenes = lax.axis_size("seq"), lax.axis_size("scene")
     capacity = 2 * rows // seqs
     count = queries.shape[0]
-    params = pltpu.CompilerParams(vmem_limit_bytes=56 * 1024 * 1024)
+    params = pltpu.CompilerParams(vmem_limit_bytes=32 * 1024 * 1024)
     prev_half = lax.ppermute(points[half:], "seq", [(i, (i + 1) % seqs) for i in range(seqs)])
     next_half = lax.ppermute(points[:half], "seq", [((i + 1) % seqs, i) for i in range(seqs)])
+    smem = pl.BlockSpec(memory_space=pltpu.SMEM)
+    kept = [pltpu.VMEM((2, half, C), BF16), pltpu.VMEM((2, 2, half, C), BF16)]
+    own = pl.pallas_call(
+        own_kernel,
+        out_shape=(
+            jax.ShapeDtypeStruct((2, half, C), BF16),
+            jax.ShapeDtypeStruct((2, 2, half, C), F32),
+            jax.ShapeDtypeStruct((2, half, 128), F32),
+            jax.ShapeDtypeStruct((2,), F32),
+        ),
+        in_specs=vmem(2),
+        out_specs=tuple(vmem(3)) + (smem,),
+        scratch_shapes=kept,
+        compiler_params=params,
+        cost_estimate=pl.CostEstimate(flops=10**10, bytes_accessed=4 * 10**6, transcendentals=8 * 10**6),
+        name="own",
+    )(points, qkv_weight)
     normed, outgoing = pl.pallas_call(
         functools.partial(block_kernel, seqs),
         out_shape=(
             jax.ShapeDtypeStruct((rows, C), BF16),
             jax.ShapeDtypeStruct((seqs, capacity + AUX, C), BF16),
         ),
-        in_specs=vmem(8),
+        in_specs=vmem(11) + [smem],
         out_specs=tuple(vmem(2)),
-        scratch_shapes=[
-            pltpu.VMEM((2, half, C), BF16),
-            pltpu.VMEM((2, 2 * half, C), BF16),
-            pltpu.VMEM((2, 2, 2 * half, C), BF16),
+        scratch_shapes=kept
+        + [
+            pltpu.VMEM((2, 2, half, C), F32),
             pltpu.VMEM((2, 2, half, C), F32),
             pltpu.VMEM((rows, C), BF16),
         ],
         compiler_params=params,
         name="block",
-    )(points, prev_half, next_half, serial_rank.reshape(1, rows), qkv_weight, proj_weight, up_weight, down_weight)
+    )(
+        points, prev_half, next_half, serial_rank.reshape(1, rows), qkv_weight, proj_weight, up_weight, down_weight, *own
+    )
     piece = -(-count // (8 * seqs * scenes)) * 8
     padded = piece * seqs * scenes
     return pl.pallas_call(
@@ -430,7 +493,7 @@
             for n in (scenes, scenes, seqs, seqs, seqs, seqs, scenes, scenes, seqs, seqs)
         ],
         compiler_params=pltpu.CompilerParams(
-            collective_id=0, has_side_effects=True, vmem_limit_bytes=56 * 1024 * 1024
+            collective_id=0, has_side_effects=True, vmem_limit_bytes=32 * 1024 * 1024
         ),
         name="tail",
     )(outgoing, normed, mask_bits, queries, dec_q_weight, dec_kv_weight, dec_out_weight, mask_weight)

time: 102 us -> 98.1 us (0.962); the launches traced: 102 us -> 97.1 us
  waiting for transfers between devices: 9.6 us -> 0.01 us
  Pallas kernels: 81.5 us -> 85.7 us
    pallas_call x0 -> x1, Pallas kernels: none -> 19.7 us  [body(): pl.pallas_call(own_kernel, out_shape=(jax.ShapeDtypeStruct((2, half, C),...]
    pallas_call x1, Pallas kernels: 39.5 us -> 25.5 us  [body(): pl.pallas_call(functools.partial(block_kernel, seqs), out_shape=(jax.Shap...]
    ppermute x1, waiting for transfers between devices: 4.99 us -> 0.01 us  [body(): lax.ppermute(points[:half], 'seq', [((i + 1) % seqs, i) for i in range(se...]
    ppermute x1, waiting for transfers between devices: 4.62 us -> 0.01 us  [body(): lax.ppermute(points[half:], 'seq', [(i, (i + 1) % seqs) for i in range(se...]
    pallas_call x1, Pallas kernels: 42.1 us -> 40.5 us  [body(): pl.pallas_call(functools.partial(tail_kernel, scenes, seqs), out_shape=(j...]
    unnamed x11 -> x27, local copies, waits for them, and re-layouts: 4.07 us -> 4.32 us
  transfers between devices with their start and end apart: 2 -> 2, of which waited for: 2 -> 0; matrix products, arithmetic and copies ran while one was open for 0% -> 0% of each run, Pallas kernels for 0% -> 20%
where the time goes in v3:
time: 98.1 us; the launch traced here: 97.1 us
  Pallas kernels  85.7 us (87%)
  local copies, waits for them, and re-layouts  5.38 us (5%)
  starting transfers between devices  5.12 us (5%)
    pallas_call x1, Pallas kernels, body(): pl.pallas_call(functools.partial(tail_kernel, scenes, seqs), out_shape=(j...  40.5 us
    pallas_call x1, Pallas kernels, body(): pl.pallas_call(functools.partial(block_kernel, seqs), out_shape=(jax.Shap...  25.5 us
    pallas_call x1, Pallas kernels, body(): pl.pallas_call(own_kernel, out_shape=(jax.ShapeDtypeStruct((2, half, C),...  19.7 us
    ppermute x1, starting transfers between devices, body(): lax.ppermute(points[:half], 'seq', [((i + 1) % seqs, i) for i in range(se...  5.12 us
    unnamed x27, local copies, waits for them, and re-layouts  4.32 us
  transfers between devices with their start and end apart: 2, of which 0 were waited for; matrix products, arithmetic and copies ran while one was open for 0% of the time, Pallas kernels for 20%

profile of v3, /device:TPU:1, one launch (start us, length us, event | category | flops | bytes accessed | tf_op | source)
XLA Modules:
  0.0 97.1 jit_solution(12495317743425665491)
XLA Ops:
  0.6 1.1 %fusion = (bf16[512,256]{1,0:T(8,128)(2,1)S(1)}, bf16[512,256]{1,0:T(8,128)(2,1)S(1)}) fusion(bf16[1024,256]{1,0:T(8,128)(2,1)} %x_ref.3), kind=kLoop, calls=%fused_computation | loop fusion | bytes 1048576 | tf_op jit(solution)/shard_map/slice | solution.py:433
  1.7 5.1 %collective-permute-start.1 = (bf16[512,256]{1,0:T(8,128)(2,1)S(1)}, bf16[512,256]{1,0:T(8,128)(2,1)S(1)}, u32[]{:S(2)}, u32[]{:S(2)}) collective-permute-start(bf16[512,256]{1,0:T(8,128)(2,1)S(1)} %get-tuple-element.15), channel_id=1, source_target_pairs={{1,0},{2,1},{3,2},{4,3},{5,4},{6,5},{7,6},{0,7},{9,8},{10,9},{11,1... | collective-permute-start | bytes 786440 | tf_op jit(solution)/shard_map/ppermute | solution.py:433
  6.8 0.0 collective-permute-start
  6.8 0.0 copy-start
  6.8 1.0 %copy-done = bf16[1024,256]{1,0:T(8,128)(2,1)S(1)} copy-done((bf16[1024,256]{1,0:T(8,128)(2,1)S(1)}, bf16[1024,256]{1,0:T(8,128)(2,1)}, u32[]{:S(2)}) %copy-start) | copy-done | bytes 524312
  7.9 0.0 copy-start.3
  7.9 1.0 %copy-done.3 = bf16[256,768]{1,0:T(8,128)(2,1)S(1)} copy-done((bf16[256,768]{1,0:T(8,128)(2,1)S(1)}, bf16[256,768]{1,0:T(8,128)(2,1)}, u32[]{:S(2)}) %copy-start.3) | copy-done | bytes 393240
  8.9 0.0 copy-start.1
  8.9 0.0 copy-start.2
  8.9 0.0 copy-start.8
  8.9 0.0 copy-start.11
  8.9 19.7 %own.1 = (bf16[2,512,256]{2,1,0:T(8,128)(2,1)S(1)}, f32[2,2,512,256]{3,2,1,0:T(8,128)S(1)}, f32[2,512,128]{2,1,0:T(8,128)S(1)}, f32[2]{0:T(128)S(1)}) custom-call(bf16[1024,256]{1,0:T(8,128)(2,1)S(1)} %copy-done, bf16[256,768]{1,0:T(8,128)(2,1)S(1)} %copy-done.3), custom_call_target="tpu_custom_call" | custom-call | flops 10000000000 | bytes 4000000 | tf_op jit(solution)/shard_map/own/pallas_call | solution.py:436
  28.6 0.0 collective-permute-done.1.next_ref
  28.6 0.0 collective-permute-done.prev_ref
  28.6 0.0 copy-done.1
  28.6 0.0 copy-done.2
  28.6 0.0 copy-done.8
  28.6 0.0 copy-done.11
  28.6 0.0 copy-start.4
  28.6 0.0 copy-start.5
  28.6 0.0 copy-start.6
  28.6 0.0 copy-start.7
  28.7 0.0 copy-start.9
  28.7 0.0 copy-start.10
  28.7 25.5 %block.1 = (bf16[1024,256]{1,0:T(8,128)(2,1)S(1)}, bf16[8,272,256]{2,1,0:T(8,128)(2,1)S(1)}) custom-call(bf16[1024,256]{1,0:T(8,128)(2,1)S(1)} %copy-done, bf16[512,256]{1,0:T(8,128)(2,1)S(1)} %collective-permute-done.prev_ref, bf16[512,256]{1,0:T(8,128)(2,1)S(1)} %collective-permute-done.1.next_ref, s32[1,1024]{1,0:T(1,128)S(1)} %bitcast.1, ...), custom_call_target="tpu_custom_call" | custom-call | tf_op jit(solution)/shard_map/block/pallas_call | solution.py:451
  54.2 0.0 copy-done.4
  54.2 0.0 copy-done.5
  54.2 0.0 copy-done.6
  54.2 0.0 copy-done.7
  54.3 0.0 copy-done.9
  54.3 0.0 copy-done.10
  54.3 40.5 %tail.1 = (bf16[1024,256]{1,0:T(8,128)(2,1)S(1)}, f32[200,256]{1,0:T(8,128)S(1)}, bf16[200,1024]{1,0:T(8,128)(2,1)S(1)}) custom-call(bf16[8,272,256]{2,1,0:T(8,128)(2,1)S(1)} %get-tuple-element.13.outgoing_ref, bf16[1024,256]{1,0:T(8,128)(2,1)S(1)} %get-tuple-element.14.norm_ref, s32[12,1024]{1,0:T(8,128)S(1)} %copy-done.10, bf16[200,256]{1,0:T(8,128)(2,1)S(1)} %copy-done.9, ...), custom_call_target="tpu_custom_call" | custom-call | tf_op jit(solution)/shard_map/tail/pallas_call | solution.py:472
  94.8 0.8 copy.18
  95.6 0.7 copy.19
  96.3 0.8 copy.20
Async XLA Ops:
  1.7 26.9 %collective-permute-start.1 = (bf16[512,256]{1,0:T(8,128)(2,1)S(1)}, bf16[512,256]{1,0:T(8,128)(2,1)S(1)}, u32[]{:S(2)}, u32[]{:S(2)}) collective-permute-start(bf16[512,256]{1,0:T(8,128)(2,1)S(1)} %get-tuple-element.15), channel_id=1, source_target_pairs={{1,0},{2,1},{3,2},{4,3},{5,4},{6,5},{7,6},{0,7},{9,8},{10,9},{11,1... | collective-permute-start | bytes 786440 | tf_op jit(solution)/shard_map/ppermute | solution.py:433
  6.8 21.7 %collective-permute-start = (bf16[512,256]{1,0:T(8,128)(2,1)S(1)}, bf16[512,256]{1,0:T(8,128)(2,1)S(1)}, u32[]{:S(2)}, u32[]{:S(2)}) collective-permute-start(bf16[512,256]{1,0:T(8,128)(2,1)S(1)} %get-tuple-element.16), channel_id=1, source_target_pairs={{0,1},{1,2},{2,3},{3,4},{4,5},{5,6},{6,7},{7,0},{8,9},{9,10},{10,1... | collective-permute-start | bytes 786440 | tf_op jit(solution)/shard_map/ppermute | solution.py:432
  6.8 1.0 %copy-start = (bf16[1024,256]{1,0:T(8,128)(2,1)S(1)}, bf16[1024,256]{1,0:T(8,128)(2,1)}, u32[]{:S(2)}) copy-start(bf16[1024,256]{1,0:T(8,128)(2,1)} %x_ref.3) | copy-start | bytes 1572868
  7.9 1.0 %copy-start.3 = (bf16[256,768]{1,0:T(8,128)(2,1)S(1)}, bf16[256,768]{1,0:T(8,128)(2,1)}, u32[]{:S(2)}) copy-start(bf16[256,768]{1,0:T(8,128)(2,1)} %qkv_ref.3) | copy-start | bytes 1179652
  8.9 19.7 %copy-start.1 = (bf16[256,1024]{1,0:T(8,128)(2,1)S(1)}, bf16[256,1024]{1,0:T(8,128)(2,1)}, u32[]{:S(2)}) copy-start(bf16[256,1024]{1,0:T(8,128)(2,1)} %up_ref.1) | copy-start | bytes 1572868
  8.9 19.7 %copy-start.2 = (bf16[1024,256]{1,0:T(8,128)(2,1)S(1)}, bf16[1024,256]{1,0:T(8,128)(2,1)}, u32[]{:S(2)}) copy-start(bf16[1024,256]{1,0:T(8,128)(2,1)} %down_ref.1) | copy-start | bytes 1572868
  8.9 19.7 %copy-start.8 = (bf16[256,256]{1,0:T(8,128)(2,1)S(1)}, bf16[256,256]{1,0:T(8,128)(2,1)}, u32[]{:S(2)}) copy-start(bf16[256,256]{1,0:T(8,128)(2,1)} %proj_ref.1) | copy-start | bytes 393220
  8.9 19.7 %copy-start.11 = (s32[1024]{0:T(1024)S(1)}, s32[1024]{0:T(1024)}, u32[]{:S(2)}) copy-start(s32[1024]{0:T(1024)} %param.13) | copy-start | bytes 12292
  28.6 25.6 %copy-start.4 = (bf16[256,512]{1,0:T(8,128)(2,1)S(1)}, bf16[256,512]{1,0:T(8,128)(2,1)}, u32[]{:S(2)}) copy-start(bf16[256,512]{1,0:T(8,128)(2,1)} %dkv_ref.1) | copy-start | bytes 786436
  28.6 25.6 %copy-start.5 = (bf16[256,256]{1,0:T(8,128)(2,1)S(1)}, bf16[256,256]{1,0:T(8,128)(2,1)}, u32[]{:S(2)}) copy-start(bf16[256,256]{1,0:T(8,128)(2,1)} %dq_ref.1) | copy-start | bytes 393220
  28.6 25.6 %copy-start.6 = (bf16[256,256]{1,0:T(8,128)(2,1)S(1)}, bf16[256,256]{1,0:T(8,128)(2,1)}, u32[]{:S(2)}) copy-start(bf16[256,256]{1,0:T(8,128)(2,1)} %out_w_ref.1) | copy-start | bytes 393220
  28.6 25.6 %copy-start.7 = (bf16[256,256]{1,0:T(8,128)(2,1)S(1)}, bf16[256,256]{1,0:T(8,128)(2,1)}, u32[]{:S(2)}) copy-start(bf16[256,256]{1,0:T(8,128)(2,1)} %mask_ref.1) | copy-start | bytes 393220
  28.7 25.6 %copy-start.9 = (bf16[200,256]{1,0:T(8,128)(2,1)S(1)}, bf16[200,256]{1,0:T(8,128)(2,1)}, u32[]{:S(2)}) copy-start(bf16[200,256]{1,0:T(8,128)(2,1)} %queries_ref.1) | copy-start | bytes 307204
  28.7 25.6 %copy-start.10 = (s32[12,1024]{1,0:T(8,128)S(1)}, s32[12,1024]{1,0:T(8,128)}, u32[]{:S(2)}) copy-start(s32[12,1024]{1,0:T(8,128)} %bits_ref.1) | copy-start | bytes 147460

commit v4 on v3

--- a/solution.py
+++ b/solution.py
@@ -66,7 +66,7 @@
 
 def attend(q_ref, k_s, v_s, acc_s, shift):
     keys = k_s.shape[1]
-    tile = 256
+    tile = 512
 
     def step(head, carry):
         for group in range(2):
@@ -330,7 +330,7 @@
         return copy
 
     order = sorted(range(1, seqs), key=lambda offset: (abs(offset - seqs // 2), offset))
-    first, second = len(order) * 4 // 7, len(order) * 6 // 7
+    first, second = len(order) * 3 // 7, len(order) * 5 // 7
     points = []
 
     def send_points(offsets):

time: 98.1 us -> 93.5 us (0.953)
  Pallas kernels: 85.7 us -> 81.9 us
    pallas_call x1, Pallas kernels: 40.5 us -> 38.7 us  [body(): pl.pallas_call(functools.partial(tail_kernel, scenes, seqs), out_shape=(j...]
    pallas_call x1, Pallas kernels: 19.7 us -> 18.6 us  [body(): pl.pallas_call(own_kernel, out_shape=(jax.ShapeDtypeStruct((2, half, C),...]
where the time goes in v4:
time: 93.5 us; the launch traced here: 93.2 us
  Pallas kernels  81.9 us (88%)
  local copies, waits for them, and re-layouts  5.38 us (6%)
  starting transfers between devices  5.12 us (5%)
    pallas_call x1, Pallas kernels, body(): pl.pallas_call(functools.partial(tail_kernel, scenes, seqs), out_shape=(j...  38.7 us
    pallas_call x1, Pallas kernels, body(): pl.pallas_call(functools.partial(block_kernel, seqs), out_shape=(jax.Shap...  24.6 us
    pallas_call x1, Pallas kernels, body(): pl.pallas_call(own_kernel, out_shape=(jax.ShapeDtypeStruct((2, half, C),...  18.6 us
    ppermute x1, starting transfers between devices, body(): lax.ppermute(points[:half], 'seq', [((i + 1) % seqs, i) for i in range(se...  5.12 us
    unnamed x27, local copies, waits for them, and re-layouts  4.32 us
  transfers between devices with their start and end apart: 2, of which 0 were waited for; matrix products, arithmetic and copies ran while one was open for 0% of the time, Pallas kernels for 20%

profile of v4, /device:TPU:1, one launch (start us, length us, event | category | flops | bytes accessed | tf_op | source)
XLA Modules:
  0.0 93.2 jit_solution(11107645802815496452)
XLA Ops:
  0.6 1.1 %fusion = (bf16[512,256]{1,0:T(8,128)(2,1)S(1)}, bf16[512,256]{1,0:T(8,128)(2,1)S(1)}) fusion(bf16[1024,256]{1,0:T(8,128)(2,1)} %x_ref.3), kind=kLoop, calls=%fused_computation | loop fusion | bytes 1048576 | tf_op jit(solution)/shard_map/slice | solution.py:433
  1.7 5.1 %collective-permute-start.1 = (bf16[512,256]{1,0:T(8,128)(2,1)S(1)}, bf16[512,256]{1,0:T(8,128)(2,1)S(1)}, u32[]{:S(2)}, u32[]{:S(2)}) collective-permute-start(bf16[512,256]{1,0:T(8,128)(2,1)S(1)} %get-tuple-element.15), channel_id=1, source_target_pairs={{1,0},{2,1},{3,2},{4,3},{5,4},{6,5},{7,6},{0,7},{9,8},{10,9},{11,1... | collective-permute-start | bytes 786440 | tf_op jit(solution)/shard_map/ppermute | solution.py:433
  6.8 0.0 collective-permute-start
  6.8 0.0 copy-start
  6.8 1.0 %copy-done = bf16[1024,256]{1,0:T(8,128)(2,1)S(1)} copy-done((bf16[1024,256]{1,0:T(8,128)(2,1)S(1)}, bf16[1024,256]{1,0:T(8,128)(2,1)}, u32[]{:S(2)}) %copy-start) | copy-done | bytes 524312
  7.9 0.0 copy-start.3
  7.9 1.0 %copy-done.3 = bf16[256,768]{1,0:T(8,128)(2,1)S(1)} copy-done((bf16[256,768]{1,0:T(8,128)(2,1)S(1)}, bf16[256,768]{1,0:T(8,128)(2,1)}, u32[]{:S(2)}) %copy-start.3) | copy-done | bytes 393240
  8.9 0.0 copy-start.1
  8.9 0.0 copy-start.2
  8.9 0.0 copy-start.8
  8.9 0.0 copy-start.11
  8.9 18.6 %own.1 = (bf16[2,512,256]{2,1,0:T(8,128)(2,1)S(1)}, f32[2,2,512,256]{3,2,1,0:T(8,128)S(1)}, f32[2,512,128]{2,1,0:T(8,128)S(1)}, f32[2]{0:T(128)S(1)}) custom-call(bf16[1024,256]{1,0:T(8,128)(2,1)S(1)} %copy-done, bf16[256,768]{1,0:T(8,128)(2,1)S(1)} %copy-done.3), custom_call_target="tpu_custom_call" | custom-call | flops 10000000000 | bytes 4000000 | tf_op jit(solution)/shard_map/own/pallas_call | solution.py:436
  27.5 0.0 collective-permute-done.1.next_ref
  27.5 0.0 collective-permute-done.prev_ref
  27.5 0.0 copy-done.1
  27.5 0.0 copy-done.2
  27.6 0.0 copy-done.8
  27.6 0.0 copy-done.11
  27.6 0.0 copy-start.4
  27.6 0.0 copy-start.5
  27.6 0.0 copy-start.6
  27.6 0.0 copy-start.7
  27.6 0.0 copy-start.9
  27.6 0.0 copy-start.10
  27.6 24.6 %block.1 = (bf16[1024,256]{1,0:T(8,128)(2,1)S(1)}, bf16[8,272,256]{2,1,0:T(8,128)(2,1)S(1)}) custom-call(bf16[1024,256]{1,0:T(8,128)(2,1)S(1)} %copy-done, bf16[512,256]{1,0:T(8,128)(2,1)S(1)} %collective-permute-done.prev_ref, bf16[512,256]{1,0:T(8,128)(2,1)S(1)} %collective-permute-done.1.next_ref, s32[1,1024]{1,0:T(1,128)S(1)} %bitcast.1, ...), custom_call_target="tpu_custom_call" | custom-call | tf_op jit(solution)/shard_map/block/pallas_call | solution.py:451
  52.2 0.0 copy-done.4
  52.2 0.0 copy-done.5
  52.2 0.0 copy-done.6
  52.2 0.0 copy-done.7
  52.3 0.0 copy-done.9
  52.3 0.0 copy-done.10
  52.3 38.7 %tail.1 = (bf16[1024,256]{1,0:T(8,128)(2,1)S(1)}, f32[200,256]{1,0:T(8,128)S(1)}, bf16[200,1024]{1,0:T(8,128)(2,1)S(1)}) custom-call(bf16[8,272,256]{2,1,0:T(8,128)(2,1)S(1)} %get-tuple-element.13.outgoing_ref, bf16[1024,256]{1,0:T(8,128)(2,1)S(1)} %get-tuple-element.14.norm_ref, s32[12,1024]{1,0:T(8,128)S(1)} %copy-done.10, bf16[200,256]{1,0:T(8,128)(2,1)S(1)} %copy-done.9, ...), custom_call_target="tpu_custom_call" | custom-call | tf_op jit(solution)/shard_map/tail/pallas_call | solution.py:472
  91.0 0.8 copy.18
  91.8 0.7 copy.19
  92.5 0.8 copy.20
Async XLA Ops:
  1.7 25.8 %collective-permute-start.1 = (bf16[512,256]{1,0:T(8,128)(2,1)S(1)}, bf16[512,256]{1,0:T(8,128)(2,1)S(1)}, u32[]{:S(2)}, u32[]{:S(2)}) collective-permute-start(bf16[512,256]{1,0:T(8,128)(2,1)S(1)} %get-tuple-element.15), channel_id=1, source_target_pairs={{1,0},{2,1},{3,2},{4,3},{5,4},{6,5},{7,6},{0,7},{9,8},{10,9},{11,1... | collective-permute-start | bytes 786440 | tf_op jit(solution)/shard_map/ppermute | solution.py:433
  6.8 20.7 %collective-permute-start = (bf16[512,256]{1,0:T(8,128)(2,1)S(1)}, bf16[512,256]{1,0:T(8,128)(2,1)S(1)}, u32[]{:S(2)}, u32[]{:S(2)}) collective-permute-start(bf16[512,256]{1,0:T(8,128)(2,1)S(1)} %get-tuple-element.16), channel_id=1, source_target_pairs={{0,1},{1,2},{2,3},{3,4},{4,5},{5,6},{6,7},{7,0},{8,9},{9,10},{10,1... | collective-permute-start | bytes 786440 | tf_op jit(solution)/shard_map/ppermute | solution.py:432
  6.8 1.0 %copy-start = (bf16[1024,256]{1,0:T(8,128)(2,1)S(1)}, bf16[1024,256]{1,0:T(8,128)(2,1)}, u32[]{:S(2)}) copy-start(bf16[1024,256]{1,0:T(8,128)(2,1)} %x_ref.3) | copy-start | bytes 1572868
  7.9 1.0 %copy-start.3 = (bf16[256,768]{1,0:T(8,128)(2,1)S(1)}, bf16[256,768]{1,0:T(8,128)(2,1)}, u32[]{:S(2)}) copy-start(bf16[256,768]{1,0:T(8,128)(2,1)} %qkv_ref.3) | copy-start | bytes 1179652
  8.9 18.7 %copy-start.1 = (bf16[256,1024]{1,0:T(8,128)(2,1)S(1)}, bf16[256,1024]{1,0:T(8,128)(2,1)}, u32[]{:S(2)}) copy-start(bf16[256,1024]{1,0:T(8,128)(2,1)} %up_ref.1) | copy-start | bytes 1572868
  8.9 18.7 %copy-start.2 = (bf16[1024,256]{1,0:T(8,128)(2,1)S(1)}, bf16[1024,256]{1,0:T(8,128)(2,1)}, u32[]{:S(2)}) copy-start(bf16[1024,256]{1,0:T(8,128)(2,1)} %down_ref.1) | copy-start | bytes 1572868
  8.9 18.7 %copy-start.8 = (bf16[256,256]{1,0:T(8,128)(2,1)S(1)}, bf16[256,256]{1,0:T(8,128)(2,1)}, u32[]{:S(2)}) copy-start(bf16[256,256]{1,0:T(8,128)(2,1)} %proj_ref.1) | copy-start | bytes 393220
  8.9 18.7 %copy-start.11 = (s32[1024]{0:T(1024)S(1)}, s32[1024]{0:T(1024)}, u32[]{:S(2)}) copy-start(s32[1024]{0:T(1024)} %param.13) | copy-start | bytes 12292
  27.6 24.6 %copy-start.4 = (bf16[256,512]{1,0:T(8,128)(2,1)S(1)}, bf16[256,512]{1,0:T(8,128)(2,1)}, u32[]{:S(2)}) copy-start(bf16[256,512]{1,0:T(8,128)(2,1)} %dkv_ref.1) | copy-start | bytes 786436
  27.6 24.6 %copy-start.5 = (bf16[256,256]{1,0:T(8,128)(2,1)S(1)}, bf16[256,256]{1,0:T(8,128)(2,1)}, u32[]{:S(2)}) copy-start(bf16[256,256]{1,0:T(8,128)(2,1)} %dq_ref.1) | copy-start | bytes 393220
  27.6 24.6 %copy-start.6 = (bf16[256,256]{1,0:T(8,128)(2,1)S(1)}, bf16[256,256]{1,0:T(8,128)(2,1)}, u32[]{:S(2)}) copy-start(bf16[256,256]{1,0:T(8,128)(2,1)} %out_w_ref.1) | copy-start | bytes 393220
  27.6 24.6 %copy-start.7 = (bf16[256,256]{1,0:T(8,128)(2,1)S(1)}, bf16[256,256]{1,0:T(8,128)(2,1)}, u32[]{:S(2)}) copy-start(bf16[256,256]{1,0:T(8,128)(2,1)} %mask_ref.1) | copy-start | bytes 393220
  27.6 24.6 %copy-start.9 = (bf16[200,256]{1,0:T(8,128)(2,1)S(1)}, bf16[200,256]{1,0:T(8,128)(2,1)}, u32[]{:S(2)}) copy-start(bf16[200,256]{1,0:T(8,128)(2,1)} %queries_ref.1) | copy-start | bytes 307204
  27.6 24.6 %copy-start.10 = (s32[12,1024]{1,0:T(8,128)S(1)}, s32[12,1024]{1,0:T(8,128)}, u32[]{:S(2)}) copy-start(s32[12,1024]{1,0:T(8,128)} %bits_ref.1) | copy-start | bytes 147460
